TPU v7x, 32 devices: a whole 2x2x4 slice. The times are simulated.
32 devices in a mesh: light: 4 (over y, x), depth: 2 (over core), height: 4 (over z).
Axes of the slice: x: 2, y: 2, z: 4, core: 2. Of those that a mesh axis runs over, the one named last changes fastest.
Arguments:
- density: float32 [64, 32, 2048], P('light', 'depth', 'height'), may hold values from 0 to 6.4
- active_list: int32 [4, 48], P('depth'), may hold values from -1 to 63, as said below
- light_dir: int32 [8], replicated, may hold values from 0 to 1, as said below
- lamp_plane: float32 [8, 32, 2048], P(None, 'depth', 'height'), may hold values from 0.5 to 2
- extinction: float32 [8], replicated, may hold values from 0.015625 to 0.078125
- blur_weights: float32 [8, 25], replicated, may hold values from 0.2 to 16
- albedo: float32 [8], replicated, may hold values from 0.3 to 1
Outputs:
- rendered: float32 [8, 64, 2048], P('depth', 'light', 'height')
Inputs may be any that keep to these rules, and one draw needn't show every extreme that they name: `active_list`: each row lists distinct brick numbers lb * 16 + hb (lb the light slab of 16 slices, hb the height brick of 128 cells) of one depth slab of 8 cells, then -1 to its end; a row lists between 24 and 48 bricks, and some row lists 48. `light_dir`: exactly 4 entries are 1.
All inputs are finite; a program needn't handle non-finite values.
Results may differ from a plain program's by a relative error of at most 0.00016.
Values sent between devices are 32-bit elements; how exact they have to be, the bound alone decides.
No kernel may reach another device: no remote copies, remote signals or barrier semaphores. Data moves between devices by JAX's collectives and lax.ppermute only.
A program may use at most 64 MiB of HBM per device.

v0:
```python
import jax
import jax.numpy as jnp
from jax import lax
from jax.experimental import pallas as pl
from jax.experimental.pallas import tpu as pltpu
from jax.sharding import PartitionSpec as P

BZ = 8
LANES = 128
TAPS = 5
GRANT = pltpu.CompilerParams(vmem_limit_bytes=24 << 20)
SMEM = pl.BlockSpec(memory_space=pltpu.SMEM)
VMEM = pl.BlockSpec(memory_space=pltpu.VMEM)
HBM = pl.BlockSpec(memory_space=pltpu.HBM)


def pairs_even(count):
    return [(i, i ^ 1) for i in range(count) if (i ^ 1) < count]


def pairs_odd(count):
    inner = [(i, i + 1) for i in range(1, count - 1, 2)]
    return inner + [(b, a) for a, b in inner]


def peer(position, k, count):
    if count & (count - 1) == 0:
        return position ^ k
    return (position - k) % count


def light_pairs(k, count):
    return [(peer(i, k, count), i) for i in range(count)]


def lane_iota(shape):
    return lax.broadcasted_iota(jnp.int32, shape, len(shape) - 1)


def in_vmem(*values):
    return [pltpu.with_memory_space_constraint(v, pltpu.VMEM) for v in values]


def in_hbm(*values):
    return [pltpu.with_memory_space_constraint(v, pltpu.HBM) for v in values]


def in_smem(*values):
    return [pltpu.with_memory_space_constraint(v, pltpu.SMEM) for v in values]


def split(value):
    high = value.astype(jnp.bfloat16)
    return high, (value - high.astype(jnp.float32)).astype(jnp.bfloat16)


def local(density, active_list, light_dir, lamp_plane, extinction, blur_weights, albedo):
    colours = extinction.shape[0]
    slices, depth_len, height_len = density.shape
    chain = lax.axis_size("light")
    groups = lax.axis_size("depth")
    columns = lax.axis_size("height")
    assert groups == 2
    mine = colours // groups
    full = depth_len * groups
    halo = 2 * (chain - 1)
    assert 2 * halo <= LANES
    wide = height_len + LANES
    per_tile = LANES // halo
    tiles = -(-(1 + colours) // per_tile)
    assert 2 * tiles * LANES <= wide * chain
    blocks = height_len // LANES
    slabs = depth_len // BZ
    halo_rows = -(-2 * tiles * LANES // wide) * depth_len

    def place(g):
        return g // per_tile, (g % per_tile) * halo

    def sums_kernel(
        density_hbm, active_hbm, lamp_hbm, dir_hbm, ext_hbm, blur_hbm, albedo_hbm,
        bundle_ref, column_ref, even_ref, odd_ref, dir_ref, ext_ref, blur_ref, albedo_ref,
        density_ref, active_ref, lamp_ref, arrivals,
    ):
        light = lax.axis_index("light")
        depth = lax.axis_index("depth")
        height = lax.axis_index("height")
        size = slices
        chunks = [pl.ds(x, min(size, slices - x)) for x in range(0, slices, size)]
        moves = [
            pltpu.make_async_copy(source, target, arrivals.at[i])
            for i, (source, target) in enumerate(
                (
                    (active_hbm, active_ref),
                    *((density_hbm.at[part], density_ref.at[part]) for part in chunks),
                    (lamp_hbm, lamp_ref),
                    (lamp_hbm.at[pl.ds((1 - depth) * mine, mine)], bundle_ref.at[pl.ds(slices, mine)]),
                    (dir_hbm, dir_ref),
                    (ext_hbm, ext_ref),
                    (blur_hbm, blur_ref),
                    (albedo_hbm, albedo_ref),
                )
            )
        ]
        for move in moves:
            move.start()
        moves[0].wait()
        listed = active_ref[...]
        first_brick = (light * columns + height) * blocks
        lives = []
        for j in range(blocks):
            hit = jnp.max(
                jnp.where(listed == first_brick + j, 1.0, 0.0), axis=1, keepdims=True
            )
            lives.append(
                jnp.concatenate(
                    [jnp.broadcast_to(hit[r : r + 1], (BZ, LANES)) for r in range(slabs)], axis=0
                )
            )
        sums = [None] * blocks
        for part, move in zip(chunks, moves[1:]):
            move.wait()
            for x in range(part.start, part.start + part.size):
                for j in range(blocks):
                    span = pl.ds(j * LANES, LANES)
                    cell = density_ref[x, :, span] * lives[j]
                    bundle_ref[x, :, span] = cell
                    sums[j] = cell if x == 0 else sums[j] + cell
        for j in range(blocks):
            column_ref[:, pl.ds(j * LANES, LANES)] = sums[j]
        moves[1 + len(chunks)].wait()
        lane = lane_iota((depth_len, LANES))
        low = [jnp.zeros((depth_len, LANES), jnp.float32) for _ in range(tiles)]
        high = [jnp.zeros((depth_len, LANES), jnp.float32) for _ in range(tiles)]
        for g in range(1 + colours):
            tile, shift = place(g)
            if g == 0:
                left, right = sums[0], sums[-1]
            else:
                owner = depth if g <= mine else 1 - depth
                c = owner * mine + (g - 1) % mine
                left = lamp_ref[c, :, pl.ds(0, LANES)]
                right = lamp_ref[c, :, pl.ds(height_len - LANES, LANES)]
            if shift:
                left = pltpu.roll(left, shift, 1)
                right = pltpu.roll(right, LANES - shift, 1)
            low[tile] = jnp.where((lane >= shift) & (lane < shift + halo), left, low[tile])
            high[tile] = jnp.where(
                (lane >= LANES - shift - halo) & (lane < LANES - shift), right, high[tile]
            )
        even_place = height % 2 == 0
        for t in range(tiles):
            span = pl.ds(t * LANES, LANES)
            even_ref[:, span] = jnp.where(even_place, high[t], low[t])
            odd_ref[:, span] = jnp.where(even_place, low[t], high[t])
        for move in moves[2 + len(chunks) :]:
            move.wait()

    bundle, column, edge_even, edge_odd, dirs, exts, blurs, albedos = pl.pallas_call(
        sums_kernel,
        name="sums",
        compiler_params=GRANT,
        in_specs=[HBM] * 7,
        out_specs=[VMEM] * 4 + [SMEM] * 4,
        out_shape=(
            pltpu.VMEM((slices + mine, depth_len, height_len), jnp.float32),
            pltpu.VMEM((depth_len, height_len), jnp.float32),
            pltpu.VMEM((depth_len, tiles * LANES), jnp.float32),
            pltpu.VMEM((depth_len, tiles * LANES), jnp.float32),
            pltpu.SMEM(light_dir.shape, jnp.int32),
            pltpu.SMEM(extinction.shape, jnp.float32),
            pltpu.SMEM(blur_weights.shape, jnp.float32),
            pltpu.SMEM(albedo.shape, jnp.float32),
        ),
        scratch_shapes=[
            pltpu.VMEM(density.shape, jnp.float32),
            pltpu.VMEM(active_list.shape, jnp.int32),
            pltpu.VMEM(lamp_plane.shape, jnp.float32),
            pltpu.SemaphoreType.DMA((8,)),
        ],
    )(*in_hbm(density, active_list, lamp_plane, light_dir, extinction, blur_weights, albedo))

    swap = [(0, 1), (1, 0)]
    theirs = lax.ppermute(bundle, "depth", swap)
    got_even = lax.ppermute(edge_even, "height", pairs_even(columns))
    got_odd = lax.ppermute(edge_odd, "height", pairs_odd(columns))

    def gains_body(dir_ref, ext_ref, cells_ref, gain_ref, through_ref, cells, earlier):
        depth = lax.axis_index("depth")
        for j in range(blocks):
            running = jnp.zeros((depth_len, LANES), jnp.float32)
            for x in range(slices):
                rows = pl.ds(x * depth_len, depth_len)
                cell = cells_ref[x, :, pl.ds(j * LANES, LANES)]
                cells[j, rows, :] = cell
                earlier[j, rows, :] = running
                running = running + cell
            earlier[j, pl.ds(slices * depth_len, depth_len), :] = running
        down = [dir_ref[depth * mine + i] == 1 for i in range(mine)]
        rate = [-ext_ref[depth * mine + i] for i in range(mine)]

        def one_depth(z, through):
            passed = []
            for j in range(blocks):
                span = pl.ds(j * LANES, LANES)
                cell = cells[j, pl.ds(z, slices, stride=depth_len), :]
                before_up = earlier[j, pl.ds(z, slices, stride=depth_len), :]
                total = earlier[j, pl.ds(slices * depth_len + z, 1), :]
                before_down = total - before_up - cell
                kept = jnp.exp(cell * (-6.0 / full))
                weight = through[j] * (1.0 - kept)
                for i in range(mine):
                    before = jnp.where(down[i], before_down, before_up)
                    gain_ref[i, z, :, span] = weight * jnp.exp(rate[i] * before)
                passed.append(through[j] * kept)
            return tuple(passed)

        start = tuple(jnp.ones((slices, LANES), jnp.float32) for _ in range(blocks))
        for j, value in enumerate(lax.fori_loop(0, depth_len, one_depth, start)):
            through_ref[:, pl.ds(j * LANES, LANES)] = value

    gains_shape = (
        pltpu.VMEM((mine, depth_len, slices, height_len), jnp.float32),
        pltpu.VMEM((slices, height_len), jnp.float32),
    )
    gains_scratch = [
        pltpu.VMEM((blocks, slices * depth_len, LANES), jnp.float32),
        pltpu.VMEM((blocks, (slices + 1) * depth_len, LANES), jnp.float32),
    ]

    def near_kernel(dir_ref, ext_ref, blur_ref, cells_ref, gain_ref, through_ref, taps_ref, *scratch):
        depth = lax.axis_index("depth")
        shape = (full, LANES)
        lane = lane_iota(shape)
        offset = lane % full - lax.broadcasted_iota(jnp.int32, shape, 0) + TAPS // 2
        for i in range(mine):
            c = depth * mine + i
            norm = blur_ref[c, 0]
            for tap in range(1, TAPS * TAPS):
                norm = norm + blur_ref[c, tap]
            inverse = 1.0 / jnp.full(shape, norm, jnp.float32)
            for b in range(TAPS):
                band = jnp.zeros(shape, jnp.float32)
                for a in range(TAPS):
                    band = jnp.where(offset == a, blur_ref[c, a * TAPS + b], band)
                band = band * inverse
                high = band.astype(jnp.bfloat16).astype(jnp.float32)
                band = jnp.where(lane < 2 * full, high, band - high)
                taps_ref[i, pl.ds(b * full, full), :] = band.astype(jnp.bfloat16)[:, : 3 * full]
        gains_body(dir_ref, ext_ref, cells_ref, gain_ref, through_ref, *scratch)

    gain_near, through_near, taps = pl.pallas_call(
        near_kernel,
        name="near_gains",
        compiler_params=GRANT,
        in_specs=[SMEM] * 3 + [VMEM],
        out_shape=gains_shape + (pltpu.VMEM((mine, TAPS * full, 3 * full), jnp.bfloat16),),
        scratch_shapes=gains_scratch,
    )(*in_smem(dirs, exts, blurs), *in_vmem(bundle))

    def widen_kernel(column_ref, even_ref, odd_ref, wide_ref, halos_ref):
        even_place = lax.axis_index("height") % 2 == 0
        lane = lane_iota((depth_len, LANES))
        for t in range(tiles):
            span = pl.ds(t * LANES, LANES)
            a, b = even_ref[:, span], odd_ref[:, span]
            from_right = jnp.where(even_place, a, b)
            from_left = jnp.where(even_place, b, a)
            halos_ref[:, span] = from_right
            halos_ref[:, pl.ds((tiles + t) * LANES, LANES)] = from_left
            if t == 0:
                edge = jnp.where(
                    lane < halo, from_right, jnp.where(lane >= LANES - halo, from_left, 0.0)
                )
                wide_ref[:, pl.ds(height_len, LANES)] = edge
        wide_ref[:, pl.ds(0, height_len)] = column_ref[...]

    wide_column, halos = pl.pallas_call(
        widen_kernel,
        name="widen",
        compiler_params=GRANT,
        out_shape=(
            pltpu.VMEM((depth_len, wide), jnp.float32),
            pltpu.VMEM((depth_len, 2 * tiles * LANES), jnp.float32),
        ),
    )(*in_vmem(column, got_even, got_odd))

    near = []
    for k in range(1, chain):
        near.append(lax.ppermute(wide_column, "light", light_pairs(k, chain)))

    gain_far, through_far = pl.pallas_call(
        gains_body,
        name="far_gains",
        compiler_params=GRANT,
        in_specs=[SMEM] * 2 + [VMEM],
        out_shape=gains_shape,
        scratch_shapes=gains_scratch,
    )(*in_smem(dirs, exts), *in_vmem(theirs))

    joined = (chain - 2) * depth_len

    def join_kernel(*refs):
        out_ref = refs[-1]
        for k, ref in enumerate(refs[: chain - 2]):
            out_ref[pl.ds(k * depth_len, depth_len), :] = ref[...]
        for t in range(2 * tiles):
            row, lane = divmod(t * LANES, wide)
            out_ref[pl.ds(joined + row * depth_len, depth_len), pl.ds(lane, LANES)] = refs[
                chain - 2
            ][:, pl.ds(t * LANES, LANES)]

    parcel = pl.pallas_call(
        join_kernel,
        name="join",
        compiler_params=GRANT,
        out_shape=pltpu.VMEM((joined + halo_rows, wide), jnp.float32),
    )(*in_vmem(*near[1:], halos))
    far_parcel = lax.ppermute(parcel, "depth", swap)
    far_last = lax.ppermute(near[0], "depth", swap)

    def chain_kernel(
        dir_ref, ext_ref, albedo_ref, lamp_ref, theirs_ref, near_last_ref, far_last_ref,
        near_ref, far_ref, taps_ref,
        gain_near_ref, through_near_ref, gain_far_ref, through_far_ref, out_ref, walls, plane, lit,
    ):
        light = lax.axis_index("light")
        depth = lax.axis_index("depth")
        height = lax.axis_index("height")
        own_row = pl.multiple_of(depth * depth_len, BZ)
        other_row = pl.multiple_of((1 - depth) * depth_len, BZ)
        for k in range(1, chain):
            source = peer(light, k, chain)
            for row, last, others in (
                (own_row, near_last_ref, near_ref),
                (other_row, far_last_ref, far_ref),
            ):
                if k > 1:
                    column = others[pl.ds((k - 2) * depth_len, depth_len), :]
                else:
                    column = last[...]
                walls[source, pl.ds(row, depth_len), :] = column
        lane = lane_iota((depth_len, LANES))

        def halo_tile(ref, t):
            row, first = divmod(t * LANES, wide)
            return ref[pl.ds(joined + row * depth_len, depth_len), pl.ds(first, LANES)]

        down = [dir_ref[depth * mine + i] for i in range(mine)]
        ups = mine - sum(down[1:], down[0])
        rank, ups_seen, downs_seen = [], 0, 0
        for i in range(mine):
            rank.append(jnp.where(down[i] == 1, ups + downs_seen, ups_seen))
            ups_seen = ups_seen + 1 - down[i]
            downs_seen = downs_seen + down[i]
        order = [
            sum((jnp.where(rank[i] == r, i, 0) for i in range(1, mine)), jnp.int32(0))
            for r in range(mine)
        ]
        for i in range(mine):
            for row, group, edges, body in (
                (own_row, 1 + i, near_ref, lamp_ref[depth * mine + i]),
                (other_row, 1 + mine + i, far_ref, theirs_ref[slices + i]),
            ):
                tile, shift = place(group)
                from_right = halo_tile(edges, tile)
                from_left = halo_tile(edges, tiles + tile)
                if shift:
                    from_right = pltpu.roll(from_right, LANES - shift, 1)
                    from_left = pltpu.roll(from_left, shift, 1)
                edge = jnp.where(
                    lane < halo, from_right, jnp.where(lane >= LANES - halo, from_left, 0.0)
                )
                plane[rank[i], pl.ds(row, depth_len), pl.ds(0, height_len)] = body
                plane[rank[i], pl.ds(row, depth_len), pl.ds(height_len, LANES)] = edge
        wide_lane = lane_iota((1, wide))
        inside = (
            (wide_lane < height_len)
            | ((wide_lane < height_len + LANES // 2) & (height < columns - 1))
            | ((wide_lane >= height_len + LANES // 2) & (height > 0))
        )
        inside = jnp.where(inside, 1.0, 0.0)
        ups_steps, down_steps = light, chain - 1 - light
        shared = jnp.minimum(ups_steps, down_steps)
        longest = jnp.maximum(ups_steps, down_steps)
        ups_longer = ups_steps > down_steps
        alone = jnp.where(ups_longer, ups, mine - ups)
        first_alone = jnp.where(ups_longer, 0, ups)
        as_pair = alone <= 2

        def advance(places, s):
            results = []
            for place_in in places:
                c = depth * mine + order[place_in] if isinstance(place_in, int) else None
                if c is None:
                    c = depth * mine + chosen(place_in)
                goes_down = place_in >= ups
                wall = walls[jnp.where(goes_down, chain - 1 - s, s)]
                before = plane[place_in]
                high, low = split(before * (jnp.exp(-ext_ref[c] * wall) * inside))
                bands = jnp.dot(
                    taps_ref[c - depth * mine],
                    jnp.concatenate([high, low, high], axis=0),
                    preferred_element_type=jnp.float32,
                )
                after = None
                for b in range(TAPS):
                    part = bands[b * full : (b + 1) * full]
                    if b != TAPS // 2:
                        part = pltpu.roll(part, (TAPS // 2 - b) % wide, 1)
                    after = part if after is None else after + part
                active = s < jnp.where(goes_down, down_steps, ups_steps)
                results.append(jnp.where(active, after, before))
            for place_in, after in zip(places, results):
                plane[place_in] = after

        def chosen(place_in):
            c = order[0]
            for i in range(1, mine):
                c = jnp.where(place_in == i, order[i], c)
            return c

        def all_step(s, carry):
            advance(range(mine), s)
            return carry

        def pair_step(s, carry):
            advance((first_alone, first_alone + jnp.maximum(alone - 1, 0)), s)
            return carry

        lax.fori_loop(0, jnp.where(as_pair, shared, longest), all_step, 0)
        lax.fori_loop(
            shared, jnp.where(as_pair & (alone > 0), longest, shared), pair_step, 0
        )
        in_front = depth == 0
        for i in range(mine):
            for half, row in enumerate((own_row, other_row)):
                lit[half, i] = plane[rank[i], pl.ds(row, depth_len), pl.ds(0, height_len)]
            shade = albedo_ref[depth * mine + i]
            sums = []
            for half, gain in enumerate((gain_near_ref, gain_far_ref)):
                parts = [None] * blocks
                for z in range(depth_len):
                    for j in range(blocks):
                        span = pl.ds(j * LANES, LANES)
                        part = lit[half, i, pl.ds(z, 1), span] * gain[i, z, :, span]
                        parts[j] = part if z == 0 else parts[j] + part
                sums.append(parts)
            for j in range(blocks):
                span = pl.ds(j * LANES, LANES)
                front = jnp.where(in_front, sums[0][j], sums[1][j])
                back = jnp.where(in_front, sums[1][j], sums[0][j])
                through = jnp.where(in_front, through_near_ref[:, span], through_far_ref[:, span])
                out_ref[i, :, span] = shade * (front + through * back)

    return pl.pallas_call(
        chain_kernel,
        name="chain",
        compiler_params=GRANT,
        in_specs=[SMEM] * 3 + [VMEM] * 11,
        out_specs=VMEM,
        out_shape=jax.ShapeDtypeStruct((mine, slices, height_len), jnp.float32),
        scratch_shapes=[
            pltpu.VMEM((chain, full, wide), jnp.float32),
            pltpu.VMEM((mine, full, wide), jnp.float32),
            pltpu.VMEM((groups, mine, depth_len, height_len), jnp.float32),
        ],
    )(
        *in_smem(dirs, exts, albedos),
        *in_vmem(lamp_plane, theirs, near[0], far_last, parcel, far_parcel, taps),
        *in_vmem(gain_near, through_near, gain_far, through_far),
    )


def solution(mesh):
    in_specs = (
        P("light", "depth", "height"),
        P("depth", None),
        P(),
        P(None, "depth", "height"),
        P(),
        P(),
        P(),
    )
    out_specs = P("depth", "light", "height")

    return jax.shard_map(local, mesh=mesh, in_specs=in_specs, out_specs=out_specs, check_vma=False)
```

profile of v0, /device:TPU:17, one launch (start us, length us, event | category | flops | bytes accessed | tf_op | source)
XLA Modules:
  0.0 24.4 jit_solution(9638892812904828389)
XLA Ops:
  0.0 0.0 copy-start
  0.0 1.4 %sums.1 = (f32[20,16,512]{2,1,0:T(8,128)S(1)}, f32[16,512]{1,0:T(8,128)S(1)}, f32[16,128]{1,0:T(8,128)S(1)}, f32[16,128]{1,0:T(8,128)S(1)}, s32[8]{0:T(128)S(4)}...) custom-call(f32[16,16,512]{2,1,0:T(8,128)} %density_hbm.1, s32[2,48]{1,0:T(2,128)} %active_hbm.1, ...), custom_call_target="tpu_custom_call" | custom-call | tf_op jit(solution)/shard_map/sums/pallas_call | solution.py:158
  1.4 0.7 %collective-permute-start = (f32[20,16,512]{2,1,0:T(8,128)S(1)}, f32[20,16,512]{2,1,0:T(8,128)S(1)}, u32[]{:S(2)}, u32[]{:S(2)}) collective-permute-start(f32[20,16,512]{2,1,0:T(8,128)S(1)} %get-tuple-element.23.cells_ref), channel_id=1, source_target_pairs={{0,4},{4,0},{1,5},{5,1},{2,6},{6,2},{3,7},{7,3},{8,12},{12,8},{9,1... | collective-permute-start | bytes 1966088 | tf_op jit(solution)/shard_map/ppermute | solution.py:183
  2.1 1.3 %collective-permute-start.1 = (f32[16,128]{1,0:T(8,128)S(1)}, f32[16,128]{1,0:T(8,128)S(1)}, u32[]{:S(2)}, u32[]{:S(2)}) collective-permute-start(f32[16,128]{1,0:T(8,128)S(1)} %get-tuple-element.25), channel_id=1, source_target_pairs={{0,1},{1,0},{2,3},{3,2},{4,5},{5,4},{6,7},{7,6},{8,9},{9,8},{10,11... | collective-permute-start | bytes 24584 | tf_op jit(solution)/shard_map/ppermute | solution.py:184
  3.4 1.9 %collective-permute-start.2 = (f32[16,128]{1,0:T(8,128)S(1)}, f32[16,128]{1,0:T(8,128)S(1)}, u32[]{:S(2)}, u32[]{:S(2)}) collective-permute-start(f32[16,128]{1,0:T(8,128)S(1)} %get-tuple-element.26), channel_id=1, source_target_pairs={{1,2},{2,1},{5,6},{6,5},{9,10},{10,9},{13,14},{14,13},{17,18},{18,... | collective-permute-start | bytes 24584 | tf_op jit(solution)/shard_map/ppermute | solution.py:185
  5.3 0.0 collective-permute-done.1.even_ref
  5.3 2.5 %collective-permute-done.2.odd_ref = f32[16,128]{1,0:T(8,128)S(1)} collective-permute-done((f32[16,128]{1,0:T(8,128)S(1)}, f32[16,128]{1,0:T(8,128)S(1)}, u32[]{:S(2)}, u32[]{:S(2)}) %collective-permute-start.2) | collective-permute-done | bytes 8224 | tf_op jit(solution)/shard_map/ppermute | solution.py:185
  7.8 1.3 %collective-permute-start.5 = (f32[16,640]{1,0:T(8,128)S(1)}, f32[16,640]{1,0:T(8,128)S(1)}, u32[]{:S(2)}, u32[]{:S(2)}) collective-permute-start(f32[16,640]{1,0:T(8,128)S(1)} %get-tuple-element.27), channel_id=1, source_target_pairs={{16,0},{24,8},{0,16},{8,24},{17,1},{25,9},{1,17},{9,25},{18,2},{26... | collective-permute-start | bytes 122888 | tf_op jit(solution)/shard_map/ppermute | solution.py:289
  9.1 1.2 %collective-permute-start.6 = (f32[16,640]{1,0:T(8,128)S(1)}, f32[16,640]{1,0:T(8,128)S(1)}, u32[]{:S(2)}, u32[]{:S(2)}) collective-permute-start(f32[16,640]{1,0:T(8,128)S(1)} %get-tuple-element.27), channel_id=1, source_target_pairs={{24,0},{16,8},{8,16},{0,24},{25,1},{17,9},{9,17},{1,25},{26,2},{18... | collective-permute-start | bytes 122888 | tf_op jit(solution)/shard_map/ppermute | solution.py:289
  10.3 0.5 %collective-permute-done.5.refs_0_ = f32[16,640]{1,0:T(8,128)S(1)} collective-permute-done((f32[16,640]{1,0:T(8,128)S(1)}, f32[16,640]{1,0:T(8,128)S(1)}, u32[]{:S(2)}, u32[]{:S(2)}) %collective-permute-start.5) | collective-permute-done | bytes 40992 | tf_op jit(solution)/shard_map/ppermute | solution.py:289
  10.7 2.2 %collective-permute-done.6.refs_1_ = f32[16,640]{1,0:T(8,128)S(1)} collective-permute-done((f32[16,640]{1,0:T(8,128)S(1)}, f32[16,640]{1,0:T(8,128)S(1)}, u32[]{:S(2)}, u32[]{:S(2)}) %collective-permute-start.6) | collective-permute-done | bytes 40992 | tf_op jit(solution)/shard_map/ppermute | solution.py:289
  13.0 2.9 %collective-permute-start.7 = (f32[48,640]{1,0:T(8,128)S(1)}, f32[48,640]{1,0:T(8,128)S(1)}, u32[]{:S(2)}, u32[]{:S(2)}) collective-permute-start(f32[48,640]{1,0:T(8,128)S(1)} %join.1.near_ref), channel_id=1, source_target_pairs={{0,4},{4,0},{1,5},{5,1},{2,6},{6,2},{3,7},{7,3},{8,12},{12,8},{9,1... | collective-permute-start | bytes 368648 | tf_op jit(solution)/shard_map/ppermute | solution.py:318
  15.9 1.2 %collective-permute-start.3 = (f32[16,640]{1,0:T(8,128)S(1)}, f32[16,640]{1,0:T(8,128)S(1)}, u32[]{:S(2)}, u32[]{:S(2)}) collective-permute-start(f32[16,640]{1,0:T(8,128)S(1)} %get-tuple-element.27), channel_id=1, source_target_pairs={{8,0},{0,8},{24,16},{16,24},{9,1},{1,9},{25,17},{17,25},{10,2},{2,... | collective-permute-start | bytes 122888 | tf_op jit(solution)/shard_map/ppermute | solution.py:289
  17.1 1.6 %collective-permute-done.3.near_last_ref = f32[16,640]{1,0:T(8,128)S(1)} collective-permute-done((f32[16,640]{1,0:T(8,128)S(1)}, f32[16,640]{1,0:T(8,128)S(1)}, u32[]{:S(2)}, u32[]{:S(2)}) %collective-permute-start.3) | collective-permute-done | bytes 40992 | tf_op jit(solution)/shard_map/ppermute | solution.py:289
  18.7 1.2 %collective-permute-start.4 = (f32[16,640]{1,0:T(8,128)S(1)}, f32[16,640]{1,0:T(8,128)S(1)}, u32[]{:S(2)}, u32[]{:S(2)}) collective-permute-start(f32[16,640]{1,0:T(8,128)S(1)} %collective-permute-done.3.near_last_ref), channel_id=1, source_target_pairs={{0,4},{4,0},{1,5},{5,1},{2,6},{6,2},{3,7},{7,3},{8,12},{12,8},{9,1... | collective-permute-start | bytes 122888 | tf_op jit(solution)/shard_map/ppermute | solution.py:319
  20.0 1.1 %near_gains.1 = (f32[4,16,16,512]{3,2,1,0:T(8,128)S(1)}, f32[16,512]{1,0:T(8,128)S(1)}, bf16[4,160,96]{2,1,0:T(8,128)(2,1)S(1)}) custom-call(s32[8]{0:T(128)S(4)} %get-tuple-element.20.dir_ref, f32[8]{0:T(128)S(4)} %get-tuple-element.21.ext_ref, f32[8,25]{1,0:T(8,128)S(4)} %get-tuple-element.29.blur_ref, f32[20,16,512]{2,1,0:T(8,128)S(1)} %get-tuple-element.23.cells_ref), custom_call_target="tpu_custom_call" | custom-call | tf_op jit(solution)/shard_map/near_gains/pallas_call | solution.py:251
  21.1 0.0 collective-permute-done.cells_ref.theirs_ref
  21.1 0.9 %far_gains.1 = (f32[4,16,16,512]{3,2,1,0:T(8,128)S(1)}, f32[16,512]{1,0:T(8,128)S(1)}) custom-call(s32[8]{0:T(128)S(4)} %get-tuple-element.20.dir_ref, f32[8]{0:T(128)S(4)} %get-tuple-element.21.ext_ref, f32[20,16,512]{2,1,0:T(8,128)S(1)} %collective-permute-done.cells_ref.theirs_ref), custom_call_target="tpu_custom_call" | custom-call | tf_op jit(solution)/shard_map/far_gains/pallas_call | solution.py:291
  22.0 0.0 collective-permute-done.4.far_last_ref
  22.0 0.0 collective-permute-done.7.far_ref
  22.0 0.0 copy-done
  22.0 2.4 %chain.1 = f32[4,16,512]{2,1,0:T(8,128)} custom-call(s32[8]{0:T(128)S(4)} %get-tuple-element.20.dir_ref, f32[8]{0:T(128)S(4)} %get-tuple-element.21.ext_ref, f32[8]{0:T(128)S(4)} %get-tuple-element.22.albedo_ref, f32[8,16,512]{2,1,0:T(8,128)S(1)} %copy-done, f32[20,16,512]{2,1,0:T(8,128)S(1)} %collective-permute-done.cells_ref.theirs_ref, ...), custom_call_target="tpu_custom_call" | custom-call | tf_op jit(solution)/shard_map/chain/pallas_call | solution.py:455
  (2 shorter events, 0.0 us)
Async XLA Ops:
  0.0 22.0 %copy-start = (f32[8,16,512]{2,1,0:T(8,128)S(1)}, f32[8,16,512]{2,1,0:T(8,128)}, u32[]{:S(2)}) copy-start(f32[8,16,512]{2,1,0:T(8,128)} %lamp_ref.1) | copy-start | bytes 786436
  1.4 19.7 %collective-permute-start = (f32[20,16,512]{2,1,0:T(8,128)S(1)}, f32[20,16,512]{2,1,0:T(8,128)S(1)}, u32[]{:S(2)}, u32[]{:S(2)}) collective-permute-start(f32[20,16,512]{2,1,0:T(8,128)S(1)} %get-tuple-element.23.cells_ref), channel_id=1, source_target_pairs={{0,4},{4,0},{1,5},{5,1},{2,6},{6,2},{3,7},{7,3},{8,12},{12,8},{9,1... | collective-permute-start | bytes 1966088 | tf_op jit(solution)/shard_map/ppermute | solution.py:183
  2.1 3.2 %collective-permute-start.1 = (f32[16,128]{1,0:T(8,128)S(1)}, f32[16,128]{1,0:T(8,128)S(1)}, u32[]{:S(2)}, u32[]{:S(2)}) collective-permute-start(f32[16,128]{1,0:T(8,128)S(1)} %get-tuple-element.25), channel_id=1, source_target_pairs={{0,1},{1,0},{2,3},{3,2},{4,5},{5,4},{6,7},{7,6},{8,9},{9,8},{10,11... | collective-permute-start | bytes 24584 | tf_op jit(solution)/shard_map/ppermute | solution.py:184
  3.4 4.4 %collective-permute-start.2 = (f32[16,128]{1,0:T(8,128)S(1)}, f32[16,128]{1,0:T(8,128)S(1)}, u32[]{:S(2)}, u32[]{:S(2)}) collective-permute-start(f32[16,128]{1,0:T(8,128)S(1)} %get-tuple-element.26), channel_id=1, source_target_pairs={{1,2},{2,1},{5,6},{6,5},{9,10},{10,9},{13,14},{14,13},{17,18},{18,... | collective-permute-start | bytes 24584 | tf_op jit(solution)/shard_map/ppermute | solution.py:185
  7.8 2.9 %collective-permute-start.5 = (f32[16,640]{1,0:T(8,128)S(1)}, f32[16,640]{1,0:T(8,128)S(1)}, u32[]{:S(2)}, u32[]{:S(2)}) collective-permute-start(f32[16,640]{1,0:T(8,128)S(1)} %get-tuple-element.27), channel_id=1, source_target_pairs={{16,0},{24,8},{0,16},{8,24},{17,1},{25,9},{1,17},{9,25},{18,2},{26... | collective-permute-start | bytes 122888 | tf_op jit(solution)/shard_map/ppermute | solution.py:289
  9.1 3.9 %collective-permute-start.6 = (f32[16,640]{1,0:T(8,128)S(1)}, f32[16,640]{1,0:T(8,128)S(1)}, u32[]{:S(2)}, u32[]{:S(2)}) collective-permute-start(f32[16,640]{1,0:T(8,128)S(1)} %get-tuple-element.27), channel_id=1, source_target_pairs={{24,0},{16,8},{8,16},{0,24},{25,1},{17,9},{9,17},{1,25},{26,2},{18... | collective-permute-start | bytes 122888 | tf_op jit(solution)/shard_map/ppermute | solution.py:289
  13.0 9.0 %collective-permute-start.7 = (f32[48,640]{1,0:T(8,128)S(1)}, f32[48,640]{1,0:T(8,128)S(1)}, u32[]{:S(2)}, u32[]{:S(2)}) collective-permute-start(f32[48,640]{1,0:T(8,128)S(1)} %join.1.near_ref), channel_id=1, source_target_pairs={{0,4},{4,0},{1,5},{5,1},{2,6},{6,2},{3,7},{7,3},{8,12},{12,8},{9,1... | collective-permute-start | bytes 368648 | tf_op jit(solution)/shard_map/ppermute | solution.py:318
  15.9 2.9 %collective-permute-start.3 = (f32[16,640]{1,0:T(8,128)S(1)}, f32[16,640]{1,0:T(8,128)S(1)}, u32[]{:S(2)}, u32[]{:S(2)}) collective-permute-start(f32[16,640]{1,0:T(8,128)S(1)} %get-tuple-element.27), channel_id=1, source_target_pairs={{8,0},{0,8},{24,16},{16,24},{9,1},{1,9},{25,17},{17,25},{10,2},{2,... | collective-permute-start | bytes 122888 | tf_op jit(solution)/shard_map/ppermute | solution.py:289
  18.7 3.3 %collective-permute-start.4 = (f32[16,640]{1,0:T(8,128)S(1)}, f32[16,640]{1,0:T(8,128)S(1)}, u32[]{:S(2)}, u32[]{:S(2)}) collective-permute-start(f32[16,640]{1,0:T(8,128)S(1)} %collective-permute-done.3.near_last_ref), channel_id=1, source_target_pairs={{0,4},{4,0},{1,5},{5,1},{2,6},{6,2},{3,7},{7,3},{8,12},{12,8},{9,1... | collective-permute-start | bytes 122888 | tf_op jit(solution)/shard_map/ppermute | solution.py:319
where the time goes:
time: 24.6 us; the launch traced here: 24.4 us
  starting transfers between devices  11.7 us (48%)
  waiting for transfers between devices  6.81 us (28%)
  Pallas kernels  5.82 us (24%)
    ppermute x3, waiting for transfers between devices, local(): near.append(lax.ppermute(wide_column, 'light', light_pairs(k, chain)))  4.34 us
    ppermute x3, starting transfers between devices, local(): near.append(lax.ppermute(wide_column, 'light', light_pairs(k, chain)))  3.67 us
    ppermute x1, starting transfers between devices, local(): far_parcel = lax.ppermute(parcel, 'depth', swap)  2.9 us
    ppermute x1, waiting for transfers between devices, local(): got_odd = lax.ppermute(edge_odd, 'height', pairs_odd(columns))  2.46 us
    pallas_call x1, Pallas kernels, local(): pl.pallas_call(chain_kernel, name='chain', compiler_params=GRANT, in_spec...  2.41 us
    ppermute x1, starting transfers between devices, local(): got_odd = lax.ppermute(edge_odd, 'height', pairs_odd(columns))  1.91 us
    pallas_call x1, Pallas kernels, local(): pl.pallas_call(sums_kernel, name='sums', compiler_params=GRANT, in_specs=...  1.37 us
    ppermute x1, starting transfers between devices, local(): got_even = lax.ppermute(edge_even, 'height', pairs_even(columns))  1.3 us
  transfers between devices with their start and end apart: 8, of which 4 were waited for; matrix products, arithmetic and copies ran while one was open for 0% of the time, Pallas kernels for 8%

commit v1 on v0

--- a/solution.py
+++ b/solution.py
@@ -14,13 +14,8 @@
 HBM = pl.BlockSpec(memory_space=pltpu.HBM)
 
 
-def pairs_even(count):
-    return [(i, i ^ 1) for i in range(count) if (i ^ 1) < count]
-
-
-def pairs_odd(count):
-    inner = [(i, i + 1) for i in range(1, count - 1, 2)]
-    return inner + [(b, a) for a, b in inner]
+def ring(step, count):
+    return [(i, (i + step) % count) for i in range(count)]
 
 
 def peer(position, k, count):
@@ -78,7 +73,7 @@
 
     def sums_kernel(
         density_hbm, active_hbm, lamp_hbm, dir_hbm, ext_hbm, blur_hbm, albedo_hbm,
-        bundle_ref, column_ref, even_ref, odd_ref, dir_ref, ext_ref, blur_ref, albedo_ref,
+        bundle_ref, column_ref, high_ref, low_ref, dir_ref, ext_ref, blur_ref, albedo_ref,
         density_ref, active_ref, lamp_ref, arrivals,
     ):
         light = lax.axis_index("light")
@@ -147,15 +142,14 @@
             high[tile] = jnp.where(
                 (lane >= LANES - shift - halo) & (lane < LANES - shift), right, high[tile]
             )
-        even_place = height % 2 == 0
         for t in range(tiles):
             span = pl.ds(t * LANES, LANES)
-            even_ref[:, span] = jnp.where(even_place, high[t], low[t])
-            odd_ref[:, span] = jnp.where(even_place, low[t], high[t])
+            high_ref[:, span] = high[t]
+            low_ref[:, span] = low[t]
         for move in moves[2 + len(chunks) :]:
             move.wait()
 
-    bundle, column, edge_even, edge_odd, dirs, exts, blurs, albedos = pl.pallas_call(
+    bundle, column, edge_high, edge_low, dirs, exts, blurs, albedos = pl.pallas_call(
         sums_kernel,
         name="sums",
         compiler_params=GRANT,
@@ -181,8 +175,8 @@
 
     swap = [(0, 1), (1, 0)]
     theirs = lax.ppermute(bundle, "depth", swap)
-    got_even = lax.ppermute(edge_even, "height", pairs_even(columns))
-    got_odd = lax.ppermute(edge_odd, "height", pairs_odd(columns))
+    from_left = lax.ppermute(edge_high, "height", ring(1, columns))
+    from_right = lax.ppermute(edge_low, "height", ring(-1, columns))
 
     def gains_body(dir_ref, ext_ref, cells_ref, gain_ref, through_ref, cells, earlier):
         depth = lax.axis_index("depth")
@@ -257,20 +251,15 @@
         scratch_shapes=gains_scratch,
     )(*in_smem(dirs, exts, blurs), *in_vmem(bundle))
 
-    def widen_kernel(column_ref, even_ref, odd_ref, wide_ref, halos_ref):
-        even_place = lax.axis_index("height") % 2 == 0
+    def widen_kernel(column_ref, left_ref, right_ref, wide_ref, halos_ref):
         lane = lane_iota((depth_len, LANES))
         for t in range(tiles):
             span = pl.ds(t * LANES, LANES)
-            a, b = even_ref[:, span], odd_ref[:, span]
-            from_right = jnp.where(even_place, a, b)
-            from_left = jnp.where(even_place, b, a)
-            halos_ref[:, span] = from_right
-            halos_ref[:, pl.ds((tiles + t) * LANES, LANES)] = from_left
+            left, right = left_ref[:, span], right_ref[:, span]
+            halos_ref[:, span] = right
+            halos_ref[:, pl.ds((tiles + t) * LANES, LANES)] = left
             if t == 0:
-                edge = jnp.where(
-                    lane < halo, from_right, jnp.where(lane >= LANES - halo, from_left, 0.0)
-                )
+                edge = jnp.where(lane < halo, right, jnp.where(lane >= LANES - halo, left, 0.0))
                 wide_ref[:, pl.ds(height_len, LANES)] = edge
         wide_ref[:, pl.ds(0, height_len)] = column_ref[...]
 
@@ -282,7 +271,7 @@
             pltpu.VMEM((depth_len, wide), jnp.float32),
             pltpu.VMEM((depth_len, 2 * tiles * LANES), jnp.float32),
         ),
-    )(*in_vmem(column, got_even, got_odd))
+    )(*in_vmem(column, from_left, from_right))
 
     near = []
     for k in range(1, chain):

time: 24.6 us -> 23.8 us (0.967)
  the two profiles are of different devices: /device:TPU:17 before, /device:TPU:0 now
where the time goes in v1:
time: 23.8 us; the launch traced here: 23.6 us
  starting transfers between devices  10.1 us (42%)
  waiting for transfers between devices  7.63 us (32%)
  Pallas kernels  5.81 us (24%)
    ppermute x3, waiting for transfers between devices, local(): near.append(lax.ppermute(wide_column, 'light', light_pairs(k, chain)))  5.98 us
    ppermute x3, starting transfers between devices, local(): near.append(lax.ppermute(wide_column, 'light', light_pairs(k, chain)))  4.78 us
    ppermute x1, starting transfers between devices, local(): from_left = lax.ppermute(edge_high, 'height', ring(1, columns))  2.63 us
    pallas_call x1, Pallas kernels, local(): pl.pallas_call(chain_kernel, name='chain', compiler_params=GRANT, in_spec...  2.4 us
    ppermute x1, starting transfers between devices, local(): from_right = lax.ppermute(edge_low, 'height', ring(-1, columns))  2.09 us
    ppermute x1, waiting for transfers between devices, local(): from_left = lax.ppermute(edge_high, 'height', ring(1, columns))  1.65 us
    pallas_call x1, Pallas kernels, local(): pl.pallas_call(sums_kernel, name='sums', compiler_params=GRANT, in_specs=...  1.37 us
    pallas_call x1, Pallas kernels, local(): pl.pallas_call(near_kernel, name='near_gains', compiler_params=GRANT, in_...  1.08 us
  transfers between devices with their start and end apart: 8, of which 4 were waited for; matrix products, arithmetic and copies ran while one was open for 0% of the time, Pallas kernels for 9%

profile of v1, /device:TPU:0, one launch (start us, length us, event | category | flops | bytes accessed | tf_op | source)
XLA Modules:
  0.0 23.6 jit_solution(6765915357381715636)
XLA Ops:
  0.0 0.0 copy-start
  0.0 1.4 %sums.1 = (f32[20,16,512]{2,1,0:T(8,128)S(1)}, f32[16,512]{1,0:T(8,128)S(1)}, f32[16,128]{1,0:T(8,128)S(1)}, f32[16,128]{1,0:T(8,128)S(1)}, s32[8]{0:T(128)S(4)}...) custom-call(f32[16,16,512]{2,1,0:T(8,128)} %density_hbm.1, s32[2,48]{1,0:T(2,128)} %active_hbm.1, ...), custom_call_target="tpu_custom_call" | custom-call | tf_op jit(solution)/shard_map/sums/pallas_call | solution.py:152
  1.4 0.6 %collective-permute-start = (f32[20,16,512]{2,1,0:T(8,128)S(1)}, f32[20,16,512]{2,1,0:T(8,128)S(1)}, u32[]{:S(2)}, u32[]{:S(2)}) collective-permute-start(f32[20,16,512]{2,1,0:T(8,128)S(1)} %get-tuple-element.23.cells_ref), channel_id=1, source_target_pairs={{0,4},{4,0},{1,5},{5,1},{2,6},{6,2},{3,7},{7,3},{8,12},{12,8},{9,1... | collective-permute-start | bytes 1966088 | tf_op jit(solution)/shard_map/ppermute | solution.py:177
  1.9 2.6 %collective-permute-start.1 = (f32[16,128]{1,0:T(8,128)S(1)}, f32[16,128]{1,0:T(8,128)S(1)}, u32[]{:S(2)}, u32[]{:S(2)}) collective-permute-start(f32[16,128]{1,0:T(8,128)S(1)} %get-tuple-element.25), channel_id=1, source_target_pairs={{0,1},{1,2},{2,3},{3,0},{4,5},{5,6},{6,7},{7,4},{8,9},{9,10},{10,1... | collective-permute-start | bytes 24584 | tf_op jit(solution)/shard_map/ppermute | solution.py:178
  4.6 2.1 %collective-permute-start.2 = (f32[16,128]{1,0:T(8,128)S(1)}, f32[16,128]{1,0:T(8,128)S(1)}, u32[]{:S(2)}, u32[]{:S(2)}) collective-permute-start(f32[16,128]{1,0:T(8,128)S(1)} %get-tuple-element.26), channel_id=1, source_target_pairs={{0,3},{1,0},{2,1},{3,2},{4,7},{5,4},{6,5},{7,6},{8,11},{9,8},{10,9... | collective-permute-start | bytes 24584 | tf_op jit(solution)/shard_map/ppermute | solution.py:179
  6.7 1.6 %collective-permute-done.1.left_ref = f32[16,128]{1,0:T(8,128)S(1)} collective-permute-done((f32[16,128]{1,0:T(8,128)S(1)}, f32[16,128]{1,0:T(8,128)S(1)}, u32[]{:S(2)}, u32[]{:S(2)}) %collective-permute-start.1) | collective-permute-done | bytes 8224 | tf_op jit(solution)/shard_map/ppermute | solution.py:178
  8.3 0.0 collective-permute-done.2.right_ref
  8.3 1.8 %collective-permute-start.5 = (f32[16,640]{1,0:T(8,128)S(1)}, f32[16,640]{1,0:T(8,128)S(1)}, u32[]{:S(2)}, u32[]{:S(2)}) collective-permute-start(f32[16,640]{1,0:T(8,128)S(1)} %get-tuple-element.27), channel_id=1, source_target_pairs={{16,0},{24,8},{0,16},{8,24},{17,1},{25,9},{1,17},{9,25},{18,2},{26... | collective-permute-start | bytes 122888 | tf_op jit(solution)/shard_map/ppermute | solution.py:278
  10.1 1.4 %collective-permute-start.6 = (f32[16,640]{1,0:T(8,128)S(1)}, f32[16,640]{1,0:T(8,128)S(1)}, u32[]{:S(2)}, u32[]{:S(2)}) collective-permute-start(f32[16,640]{1,0:T(8,128)S(1)} %get-tuple-element.27), channel_id=1, source_target_pairs={{24,0},{16,8},{8,16},{0,24},{25,1},{17,9},{9,17},{1,25},{26,2},{18... | collective-permute-start | bytes 122888 | tf_op jit(solution)/shard_map/ppermute | solution.py:278
  11.5 0.8 %collective-permute-done.5.refs_0_ = f32[16,640]{1,0:T(8,128)S(1)} collective-permute-done((f32[16,640]{1,0:T(8,128)S(1)}, f32[16,640]{1,0:T(8,128)S(1)}, u32[]{:S(2)}, u32[]{:S(2)}) %collective-permute-start.5) | collective-permute-done | bytes 40992 | tf_op jit(solution)/shard_map/ppermute | solution.py:278
  12.4 2.6 %collective-permute-done.6.refs_1_ = f32[16,640]{1,0:T(8,128)S(1)} collective-permute-done((f32[16,640]{1,0:T(8,128)S(1)}, f32[16,640]{1,0:T(8,128)S(1)}, u32[]{:S(2)}, u32[]{:S(2)}) %collective-permute-start.6) | collective-permute-done | bytes 40992 | tf_op jit(solution)/shard_map/ppermute | solution.py:278
  15.0 0.1 collective-permute-start.7
  15.1 1.6 %collective-permute-start.3 = (f32[16,640]{1,0:T(8,128)S(1)}, f32[16,640]{1,0:T(8,128)S(1)}, u32[]{:S(2)}, u32[]{:S(2)}) collective-permute-start(f32[16,640]{1,0:T(8,128)S(1)} %get-tuple-element.27), channel_id=1, source_target_pairs={{8,0},{0,8},{24,16},{16,24},{9,1},{1,9},{25,17},{17,25},{10,2},{2,... | collective-permute-start | bytes 122888 | tf_op jit(solution)/shard_map/ppermute | solution.py:278
  16.7 2.5 %collective-permute-done.3.near_last_ref = f32[16,640]{1,0:T(8,128)S(1)} collective-permute-done((f32[16,640]{1,0:T(8,128)S(1)}, f32[16,640]{1,0:T(8,128)S(1)}, u32[]{:S(2)}, u32[]{:S(2)}) %collective-permute-start.3) | collective-permute-done | bytes 40992 | tf_op jit(solution)/shard_map/ppermute | solution.py:278
  19.2 0.0 collective-permute-start.4
  19.2 1.1 %near_gains.1 = (f32[4,16,16,512]{3,2,1,0:T(8,128)S(1)}, f32[16,512]{1,0:T(8,128)S(1)}, bf16[4,160,96]{2,1,0:T(8,128)(2,1)S(1)}) custom-call(s32[8]{0:T(128)S(4)} %get-tuple-element.20.dir_ref, f32[8]{0:T(128)S(4)} %get-tuple-element.21.ext_ref, f32[8,25]{1,0:T(8,128)S(4)} %get-tuple-element.29.blur_ref, f32[20,16,512]{2,1,0:T(8,128)S(1)} %get-tuple-element.23.cells_ref), custom_call_target="tpu_custom_call" | custom-call | tf_op jit(solution)/shard_map/near_gains/pallas_call | solution.py:245
  20.3 0.0 collective-permute-done.cells_ref.theirs_ref
  20.3 0.9 %far_gains.1 = (f32[4,16,16,512]{3,2,1,0:T(8,128)S(1)}, f32[16,512]{1,0:T(8,128)S(1)}) custom-call(s32[8]{0:T(128)S(4)} %get-tuple-element.20.dir_ref, f32[8]{0:T(128)S(4)} %get-tuple-element.21.ext_ref, f32[20,16,512]{2,1,0:T(8,128)S(1)} %collective-permute-done.cells_ref.theirs_ref), custom_call_target="tpu_custom_call" | custom-call | tf_op jit(solution)/shard_map/far_gains/pallas_call | solution.py:280
  21.2 0.0 collective-permute-done.4.far_last_ref
  21.2 0.0 collective-permute-done.7.far_ref
  21.2 0.0 copy-done
  21.2 2.4 %chain.1 = f32[4,16,512]{2,1,0:T(8,128)} custom-call(s32[8]{0:T(128)S(4)} %get-tuple-element.20.dir_ref, f32[8]{0:T(128)S(4)} %get-tuple-element.21.ext_ref, f32[8]{0:T(128)S(4)} %get-tuple-element.22.albedo_ref, f32[8,16,512]{2,1,0:T(8,128)S(1)} %copy-done, f32[20,16,512]{2,1,0:T(8,128)S(1)} %collective-permute-done.cells_ref.theirs_ref, ...), custom_call_target="tpu_custom_call" | custom-call | tf_op jit(solution)/shard_map/chain/pallas_call | solution.py:444
  (2 shorter events, 0.0 us)
Async XLA Ops:
  0.0 21.2 %copy-start = (f32[8,16,512]{2,1,0:T(8,128)S(1)}, f32[8,16,512]{2,1,0:T(8,128)}, u32[]{:S(2)}) copy-start(f32[8,16,512]{2,1,0:T(8,128)} %lamp_ref.1) | copy-start | bytes 786436
  1.4 18.9 %collective-permute-start = (f32[20,16,512]{2,1,0:T(8,128)S(1)}, f32[20,16,512]{2,1,0:T(8,128)S(1)}, u32[]{:S(2)}, u32[]{:S(2)}) collective-permute-start(f32[20,16,512]{2,1,0:T(8,128)S(1)} %get-tuple-element.23.cells_ref), channel_id=1, source_target_pairs={{0,4},{4,0},{1,5},{5,1},{2,6},{6,2},{3,7},{7,3},{8,12},{12,8},{9,1... | collective-permute-start | bytes 1966088 | tf_op jit(solution)/shard_map/ppermute | solution.py:177
  1.9 6.4 %collective-permute-start.1 = (f32[16,128]{1,0:T(8,128)S(1)}, f32[16,128]{1,0:T(8,128)S(1)}, u32[]{:S(2)}, u32[]{:S(2)}) collective-permute-start(f32[16,128]{1,0:T(8,128)S(1)} %get-tuple-element.25), channel_id=1, source_target_pairs={{0,1},{1,2},{2,3},{3,0},{4,5},{5,6},{6,7},{7,4},{8,9},{9,10},{10,1... | collective-permute-start | bytes 24584 | tf_op jit(solution)/shard_map/ppermute | solution.py:178
  4.6 3.7 %collective-permute-start.2 = (f32[16,128]{1,0:T(8,128)S(1)}, f32[16,128]{1,0:T(8,128)S(1)}, u32[]{:S(2)}, u32[]{:S(2)}) collective-permute-start(f32[16,128]{1,0:T(8,128)S(1)} %get-tuple-element.26), channel_id=1, source_target_pairs={{0,3},{1,0},{2,1},{3,2},{4,7},{5,4},{6,5},{7,6},{8,11},{9,8},{10,9... | collective-permute-start | bytes 24584 | tf_op jit(solution)/shard_map/ppermute | solution.py:179
  8.3 4.1 %collective-permute-start.5 = (f32[16,640]{1,0:T(8,128)S(1)}, f32[16,640]{1,0:T(8,128)S(1)}, u32[]{:S(2)}, u32[]{:S(2)}) collective-permute-start(f32[16,640]{1,0:T(8,128)S(1)} %get-tuple-element.27), channel_id=1, source_target_pairs={{16,0},{24,8},{0,16},{8,24},{17,1},{25,9},{1,17},{9,25},{18,2},{26... | collective-permute-start | bytes 122888 | tf_op jit(solution)/shard_map/ppermute | solution.py:278
  10.1 4.9 %collective-permute-start.6 = (f32[16,640]{1,0:T(8,128)S(1)}, f32[16,640]{1,0:T(8,128)S(1)}, u32[]{:S(2)}, u32[]{:S(2)}) collective-permute-start(f32[16,640]{1,0:T(8,128)S(1)} %get-tuple-element.27), channel_id=1, source_target_pairs={{24,0},{16,8},{8,16},{0,24},{25,1},{17,9},{9,17},{1,25},{26,2},{18... | collective-permute-start | bytes 122888 | tf_op jit(solution)/shard_map/ppermute | solution.py:278
  15.0 6.2 %collective-permute-start.7 = (f32[48,640]{1,0:T(8,128)S(1)}, f32[48,640]{1,0:T(8,128)S(1)}, u32[]{:S(2)}, u32[]{:S(2)}) collective-permute-start(f32[48,640]{1,0:T(8,128)S(1)} %join.1.near_ref), channel_id=1, source_target_pairs={{0,4},{4,0},{1,5},{5,1},{2,6},{6,2},{3,7},{7,3},{8,12},{12,8},{9,1... | collective-permute-start | bytes 368648 | tf_op jit(solution)/shard_map/ppermute | solution.py:307
  15.1 4.1 %collective-permute-start.3 = (f32[16,640]{1,0:T(8,128)S(1)}, f32[16,640]{1,0:T(8,128)S(1)}, u32[]{:S(2)}, u32[]{:S(2)}) collective-permute-start(f32[16,640]{1,0:T(8,128)S(1)} %get-tuple-element.27), channel_id=1, source_target_pairs={{8,0},{0,8},{24,16},{16,24},{9,1},{1,9},{25,17},{17,25},{10,2},{2,... | collective-permute-start | bytes 122888 | tf_op jit(solution)/shard_map/ppermute | solution.py:278
  19.2 2.0 %collective-permute-start.4 = (f32[16,640]{1,0:T(8,128)S(1)}, f32[16,640]{1,0:T(8,128)S(1)}, u32[]{:S(2)}, u32[]{:S(2)}) collective-permute-start(f32[16,640]{1,0:T(8,128)S(1)} %collective-permute-done.3.near_last_ref), channel_id=1, source_target_pairs={{0,4},{4,0},{1,5},{5,1},{2,6},{6,2},{3,7},{7,3},{8,12},{12,8},{9,1... | collective-permute-start | bytes 122888 | tf_op jit(solution)/shard_map/ppermute | solution.py:308

commit v2 on v1

--- a/solution.py
+++ b/solution.py
@@ -14,8 +14,13 @@
 HBM = pl.BlockSpec(memory_space=pltpu.HBM)
 
 
-def ring(step, count):
-    return [(i, (i + step) % count) for i in range(count)]
+def loops(lights, heights):
+    steps = []
+    for light in range(0, lights, 2):
+        loop = [light * heights + h for h in range(heights)]
+        loop += [(light + 1) * heights + h for h in reversed(range(heights))]
+        steps += list(zip(loop, loop[1:] + loop[:1]))
+    return steps
 
 
 def peer(position, k, count):
@@ -73,22 +78,19 @@
 
     def sums_kernel(
         density_hbm, active_hbm, lamp_hbm, dir_hbm, ext_hbm, blur_hbm, albedo_hbm,
-        bundle_ref, column_ref, high_ref, low_ref, dir_ref, ext_ref, blur_ref, albedo_ref,
-        density_ref, active_ref, lamp_ref, arrivals,
+        cells_ref, column_ref, along_ref, against_ref, lamp_ref, dir_ref, ext_ref, blur_ref, albedo_ref,
+        density_ref, active_ref, arrivals,
     ):
         light = lax.axis_index("light")
         depth = lax.axis_index("depth")
         height = lax.axis_index("height")
-        size = slices
-        chunks = [pl.ds(x, min(size, slices - x)) for x in range(0, slices, size)]
         moves = [
             pltpu.make_async_copy(source, target, arrivals.at[i])
             for i, (source, target) in enumerate(
                 (
                     (active_hbm, active_ref),
-                    *((density_hbm.at[part], density_ref.at[part]) for part in chunks),
+                    (density_hbm, density_ref),
                     (lamp_hbm, lamp_ref),
-                    (lamp_hbm.at[pl.ds((1 - depth) * mine, mine)], bundle_ref.at[pl.ds(slices, mine)]),
                     (dir_hbm, dir_ref),
                     (ext_hbm, ext_ref),
                     (blur_hbm, blur_ref),
@@ -112,17 +114,16 @@
                 )
             )
         sums = [None] * blocks
-        for part, move in zip(chunks, moves[1:]):
-            move.wait()
-            for x in range(part.start, part.start + part.size):
-                for j in range(blocks):
-                    span = pl.ds(j * LANES, LANES)
-                    cell = density_ref[x, :, span] * lives[j]
-                    bundle_ref[x, :, span] = cell
-                    sums[j] = cell if x == 0 else sums[j] + cell
+        moves[1].wait()
+        for x in range(slices):
+            for j in range(blocks):
+                span = pl.ds(j * LANES, LANES)
+                cell = density_ref[x, :, span] * lives[j]
+                cells_ref[x, :, span] = cell
+                sums[j] = cell if x == 0 else sums[j] + cell
         for j in range(blocks):
             column_ref[:, pl.ds(j * LANES, LANES)] = sums[j]
-        moves[1 + len(chunks)].wait()
+        moves[2].wait()
         lane = lane_iota((depth_len, LANES))
         low = [jnp.zeros((depth_len, LANES), jnp.float32) for _ in range(tiles)]
         high = [jnp.zeros((depth_len, LANES), jnp.float32) for _ in range(tiles)]
@@ -142,24 +143,26 @@
             high[tile] = jnp.where(
                 (lane >= LANES - shift - halo) & (lane < LANES - shift), right, high[tile]
             )
+        upwards = light % 2 == 0
         for t in range(tiles):
             span = pl.ds(t * LANES, LANES)
-            high_ref[:, span] = high[t]
-            low_ref[:, span] = low[t]
-        for move in moves[2 + len(chunks) :]:
+            along_ref[:, span] = jnp.where(upwards, high[t], low[t])
+            against_ref[:, span] = jnp.where(upwards, low[t], high[t])
+        for move in moves[3:]:
             move.wait()
 
-    bundle, column, edge_high, edge_low, dirs, exts, blurs, albedos = pl.pallas_call(
+    cells, column, edge_along, edge_against, lamps, dirs, exts, blurs, albedos = pl.pallas_call(
         sums_kernel,
         name="sums",
         compiler_params=GRANT,
         in_specs=[HBM] * 7,
-        out_specs=[VMEM] * 4 + [SMEM] * 4,
+        out_specs=[VMEM] * 5 + [SMEM] * 4,
         out_shape=(
-            pltpu.VMEM((slices + mine, depth_len, height_len), jnp.float32),
+            pltpu.VMEM(density.shape, jnp.float32),
             pltpu.VMEM((depth_len, height_len), jnp.float32),
             pltpu.VMEM((depth_len, tiles * LANES), jnp.float32),
             pltpu.VMEM((depth_len, tiles * LANES), jnp.float32),
+            pltpu.VMEM(lamp_plane.shape, jnp.float32),
             pltpu.SMEM(light_dir.shape, jnp.int32),
             pltpu.SMEM(extinction.shape, jnp.float32),
             pltpu.SMEM(blur_weights.shape, jnp.float32),
@@ -168,15 +171,17 @@
         scratch_shapes=[
             pltpu.VMEM(density.shape, jnp.float32),
             pltpu.VMEM(active_list.shape, jnp.int32),
-            pltpu.VMEM(lamp_plane.shape, jnp.float32),
-            pltpu.SemaphoreType.DMA((8,)),
+            pltpu.SemaphoreType.DMA((7,)),
         ],
     )(*in_hbm(density, active_list, lamp_plane, light_dir, extinction, blur_weights, albedo))
 
     swap = [(0, 1), (1, 0)]
-    theirs = lax.ppermute(bundle, "depth", swap)
-    from_left = lax.ppermute(edge_high, "height", ring(1, columns))
-    from_right = lax.ppermute(edge_low, "height", ring(-1, columns))
+    assert chain % 2 == 0
+    along = loops(chain, columns)
+    got_along = lax.ppermute(edge_along, ("light", "height"), along)
+    got_against = lax.ppermute(
+        edge_against, ("light", "height"), [(target, source) for source, target in along]
+    )
 
     def gains_body(dir_ref, ext_ref, cells_ref, gain_ref, through_ref, cells, earlier):
         depth = lax.axis_index("depth")
@@ -221,7 +226,10 @@
         pltpu.VMEM((blocks, (slices + 1) * depth_len, LANES), jnp.float32),
     ]
 
-    def near_kernel(dir_ref, ext_ref, blur_ref, cells_ref, gain_ref, through_ref, taps_ref, *scratch):
+    def near_kernel(
+        dir_ref, ext_ref, blur_ref, cells_ref, lamp_ref, gain_ref, through_ref, taps_ref, bundle_ref,
+        *scratch,
+    ):
         depth = lax.axis_index("depth")
         shape = (full, LANES)
         lane = lane_iota(shape)
@@ -240,22 +248,35 @@
                 high = band.astype(jnp.bfloat16).astype(jnp.float32)
                 band = jnp.where(lane < 2 * full, high, band - high)
                 taps_ref[i, pl.ds(b * full, full), :] = band.astype(jnp.bfloat16)[:, : 3 * full]
+        for x in range(slices):
+            bundle_ref[x] = cells_ref[x]
+        for i in range(mine):
+            bundle_ref[slices + i] = lamp_ref[(1 - depth) * mine + i]
         gains_body(dir_ref, ext_ref, cells_ref, gain_ref, through_ref, *scratch)
 
-    gain_near, through_near, taps = pl.pallas_call(
+    gain_near, through_near, taps, bundle = pl.pallas_call(
         near_kernel,
         name="near_gains",
         compiler_params=GRANT,
-        in_specs=[SMEM] * 3 + [VMEM],
-        out_shape=gains_shape + (pltpu.VMEM((mine, TAPS * full, 3 * full), jnp.bfloat16),),
+        in_specs=[SMEM] * 3 + [VMEM] * 2,
+        out_shape=gains_shape
+        + (
+            pltpu.VMEM((mine, TAPS * full, 3 * full), jnp.bfloat16),
+            pltpu.VMEM((slices + mine, depth_len, height_len), jnp.float32),
+        ),
         scratch_shapes=gains_scratch,
-    )(*in_smem(dirs, exts, blurs), *in_vmem(bundle))
-
-    def widen_kernel(column_ref, left_ref, right_ref, wide_ref, halos_ref):
+    )(*in_smem(dirs, exts, blurs), *in_vmem(cells, lamps))
+
+    theirs = lax.ppermute(bundle, "depth", swap)
+
+    def widen_kernel(column_ref, along_ref, against_ref, wide_ref, halos_ref):
+        upwards = lax.axis_index("light") % 2 == 0
         lane = lane_iota((depth_len, LANES))
         for t in range(tiles):
             span = pl.ds(t * LANES, LANES)
-            left, right = left_ref[:, span], right_ref[:, span]
+            along, against = along_ref[:, span], against_ref[:, span]
+            left = jnp.where(upwards, along, against)
+            right = jnp.where(upwards, against, along)
             halos_ref[:, span] = right
             halos_ref[:, pl.ds((tiles + t) * LANES, LANES)] = left
             if t == 0:
@@ -271,7 +292,7 @@
             pltpu.VMEM((depth_len, wide), jnp.float32),
             pltpu.VMEM((depth_len, 2 * tiles * LANES), jnp.float32),
         ),
-    )(*in_vmem(column, from_left, from_right))
+    )(*in_vmem(column, got_along, got_against))
 
     near = []
     for k in range(1, chain):
@@ -455,7 +476,7 @@
         ],
     )(
         *in_smem(dirs, exts, albedos),
-        *in_vmem(lamp_plane, theirs, near[0], far_last, parcel, far_parcel, taps),
+        *in_vmem(lamps, theirs, near[0], far_last, parcel, far_parcel, taps),
         *in_vmem(gain_near, through_near, gain_far, through_far),
     )
 

time: 23.8 us -> 22.6 us (0.950)
  starting transfers between devices: 10.1 us -> 6.56 us
  waiting for transfers between devices: 7.63 us -> 10.2 us
    ppermute x2, starting transfers between devices: 4.72 us -> 2.63 us  [the longest x1 2.62 us: local(): got_along = lax.ppermute(edge_along, ('light', 'height'), along)]
    ppermute x2, waiting for transfers between devices: 1.65 us -> 3.65 us  [the longest x1 2.11 us: local(): lax.ppermute(edge_against, ('light', 'height'), [(target, source) for sou...]
    ppermute x3, starting transfers between devices: 4.78 us -> 3.31 us  [local(): near.append(lax.ppermute(wide_column, 'light', light_pairs(k, chain)))]
    ppermute x1, waiting for transfers between devices: 0.01 us -> 0.27 us  [local(): far_last = lax.ppermute(near[0], 'depth', swap)]
    ppermute x3, waiting for transfers between devices: 5.98 us -> 6.23 us  [local(): near.append(lax.ppermute(wide_column, 'light', light_pairs(k, chain)))]
  transfers between devices with their start and end apart: 8 -> 8, of which waited for: 4 -> 6; matrix products, arithmetic and copies ran while one was open for 0% -> 0% of each run, Pallas kernels for 9% -> 4%
where the time goes in v2:
time: 22.6 us; the launch traced here: 22.5 us
  waiting for transfers between devices  10.2 us (45%)
  starting transfers between devices  6.56 us (29%)
  Pallas kernels  5.71 us (25%)
    ppermute x3, waiting for transfers between devices, local(): near.append(lax.ppermute(wide_column, 'light', light_pairs(k, chain)))  6.23 us
    ppermute x3, starting transfers between devices, local(): near.append(lax.ppermute(wide_column, 'light', light_pairs(k, chain)))  3.31 us
    ppermute x1, starting transfers between devices, local(): got_along = lax.ppermute(edge_along, ('light', 'height'), along)  2.62 us
    pallas_call x1, Pallas kernels, local(): pl.pallas_call(chain_kernel, name='chain', compiler_params=GRANT, in_spec...  2.3 us
    ppermute x1, waiting for transfers between devices, local(): lax.ppermute(edge_against, ('light', 'height'), [(target, source) for sou...  2.11 us
    ppermute x1, waiting for transfers between devices, local(): got_along = lax.ppermute(edge_along, ('light', 'height'), along)  1.54 us
    pallas_call x1, Pallas kernels, local(): pl.pallas_call(sums_kernel, name='sums', compiler_params=GRANT, in_specs=...  1.32 us
    pallas_call x1, Pallas kernels, local(): pl.pallas_call(near_kernel, name='near_gains', compiler_params=GRANT, in_...  1.13 us
  transfers between devices with their start and end apart: 8, of which 6 were waited for; matrix products, arithmetic and copies ran while one was open for 0% of the time, Pallas kernels for 4%

profile of v2, /device:TPU:0, one launch (start us, length us, event | category | flops | bytes accessed | tf_op | source)
XLA Modules:
  0.0 22.5 jit_solution(14415927319169875424)
XLA Ops:
  0.0 1.3 %sums.1 = (f32[16,16,512]{2,1,0:T(8,128)S(1)}, f32[16,512]{1,0:T(8,128)S(1)}, f32[16,128]{1,0:T(8,128)S(1)}, f32[16,128]{1,0:T(8,128)S(1)}, f32[8,16,512]{2,1,0:...) custom-call(f32[16,16,512]{2,1,0:T(8,128)} %density_hbm.1, ...), custom_call_target="tpu_custom_call" | custom-call | tf_op jit(solution)/shard_map/sums/pallas_call | solution.py:154
  1.3 1.1 %near_gains.1 = (f32[4,16,16,512]{3,2,1,0:T(8,128)S(1)}, f32[16,512]{1,0:T(8,128)S(1)}, bf16[4,160,96]{2,1,0:T(8,128)(2,1)S(1)}, f32[20,16,512]{2,1,0:T(8,128)S(1)}) custom-call(s32[8]{0:T(128)S(4)} %get-tuple-element.22.dir_ref, f32[8]{0:T(128)S(4)} %get-tuple-element.23.ext_ref, f32[8,25]{1,0:T(8,128)S(4)} %get-tuple-element.26.blur_ref, ...), custom_call_target="tpu_custom_call" | custom-call | tf_op jit(solution)/shard_map/near_gains/pallas_call | solution.py:257
  2.5 0.6 %collective-permute-start = (f32[20,16,512]{2,1,0:T(8,128)S(1)}, f32[20,16,512]{2,1,0:T(8,128)S(1)}, u32[]{:S(2)}, u32[]{:S(2)}) collective-permute-start(f32[20,16,512]{2,1,0:T(8,128)S(1)} %get-tuple-element.28), channel_id=1, source_target_pairs={{0,4},{4,0},{1,5},{5,1},{2,6},{6,2},{3,7},{7,3},{8,12},{12,8},{9,1... | collective-permute-start | bytes 1966088 | tf_op jit(solution)/shard_map/ppermute | solution.py:270
  3.0 2.6 %collective-permute-start.1 = (f32[16,128]{1,0:T(8,128)S(1)}, f32[16,128]{1,0:T(8,128)S(1)}, u32[]{:S(2)}, u32[]{:S(2)}) collective-permute-start(f32[16,128]{1,0:T(8,128)S(1)} %get-tuple-element.30), channel_id=1, source_target_pairs={{0,1},{1,2},{2,3},{3,11},{11,10},{10,9},{9,8},{8,0},{16,17},{17,18... | collective-permute-start | bytes 24584 | tf_op jit(solution)/shard_map/ppermute | solution.py:181
  5.7 0.0 collective-permute-start.2
  5.7 1.5 %collective-permute-done.1.along_ref = f32[16,128]{1,0:T(8,128)S(1)} collective-permute-done((f32[16,128]{1,0:T(8,128)S(1)}, f32[16,128]{1,0:T(8,128)S(1)}, u32[]{:S(2)}, u32[]{:S(2)}) %collective-permute-start.1) | collective-permute-done | bytes 8224 | tf_op jit(solution)/shard_map/ppermute | solution.py:181
  7.2 2.1 %collective-permute-done.2.against_ref = f32[16,128]{1,0:T(8,128)S(1)} collective-permute-done((f32[16,128]{1,0:T(8,128)S(1)}, f32[16,128]{1,0:T(8,128)S(1)}, u32[]{:S(2)}, u32[]{:S(2)}) %collective-permute-start.2) | collective-permute-done | bytes 8224 | tf_op jit(solution)/shard_map/ppermute | solution.py:182
  9.3 1.5 %collective-permute-start.6 = (f32[16,640]{1,0:T(8,128)S(1)}, f32[16,640]{1,0:T(8,128)S(1)}, u32[]{:S(2)}, u32[]{:S(2)}) collective-permute-start(f32[16,640]{1,0:T(8,128)S(1)} %get-tuple-element.32), channel_id=1, source_target_pairs={{24,0},{16,8},{8,16},{0,24},{25,1},{17,9},{9,17},{1,25},{26,2},{18... | collective-permute-start | bytes 122888 | tf_op jit(solution)/shard_map/ppermute | solution.py:299
  10.8 0.2 collective-permute-start.5
  11.0 3.3 %collective-permute-done.6.refs_1_ = f32[16,640]{1,0:T(8,128)S(1)} collective-permute-done((f32[16,640]{1,0:T(8,128)S(1)}, f32[16,640]{1,0:T(8,128)S(1)}, u32[]{:S(2)}, u32[]{:S(2)}) %collective-permute-start.6) | collective-permute-done | bytes 40992 | tf_op jit(solution)/shard_map/ppermute | solution.py:299
  14.3 0.5 %collective-permute-done.5.refs_0_ = f32[16,640]{1,0:T(8,128)S(1)} collective-permute-done((f32[16,640]{1,0:T(8,128)S(1)}, f32[16,640]{1,0:T(8,128)S(1)}, u32[]{:S(2)}, u32[]{:S(2)}) %collective-permute-start.5) | collective-permute-done | bytes 40992 | tf_op jit(solution)/shard_map/ppermute | solution.py:299
  14.8 0.1 collective-permute-start.7
  14.9 1.6 %collective-permute-start.3 = (f32[16,640]{1,0:T(8,128)S(1)}, f32[16,640]{1,0:T(8,128)S(1)}, u32[]{:S(2)}, u32[]{:S(2)}) collective-permute-start(f32[16,640]{1,0:T(8,128)S(1)} %get-tuple-element.32), channel_id=1, source_target_pairs={{8,0},{0,8},{24,16},{16,24},{9,1},{1,9},{25,17},{17,25},{10,2},{2,... | collective-permute-start | bytes 122888 | tf_op jit(solution)/shard_map/ppermute | solution.py:299
  16.5 2.4 %collective-permute-done.3.near_last_ref = f32[16,640]{1,0:T(8,128)S(1)} collective-permute-done((f32[16,640]{1,0:T(8,128)S(1)}, f32[16,640]{1,0:T(8,128)S(1)}, u32[]{:S(2)}, u32[]{:S(2)}) %collective-permute-start.3) | collective-permute-done | bytes 40992 | tf_op jit(solution)/shard_map/ppermute | solution.py:299
  18.9 0.0 collective-permute-start.4
  19.0 0.0 collective-permute-done.cells_ref.theirs_ref
  19.0 0.9 %far_gains.1 = (f32[4,16,16,512]{3,2,1,0:T(8,128)S(1)}, f32[16,512]{1,0:T(8,128)S(1)}) custom-call(s32[8]{0:T(128)S(4)} %get-tuple-element.22.dir_ref, f32[8]{0:T(128)S(4)} %get-tuple-element.23.ext_ref, f32[20,16,512]{2,1,0:T(8,128)S(1)} %collective-permute-done.cells_ref.theirs_ref), custom_call_target="tpu_custom_call" | custom-call | tf_op jit(solution)/shard_map/far_gains/pallas_call | solution.py:301
  19.9 0.3 %collective-permute-done.4.far_last_ref = f32[16,640]{1,0:T(8,128)S(1)} collective-permute-done((f32[16,640]{1,0:T(8,128)S(1)}, f32[16,640]{1,0:T(8,128)S(1)}, u32[]{:S(2)}, u32[]{:S(2)}) %collective-permute-start.4) | collective-permute-done | bytes 40992 | tf_op jit(solution)/shard_map/ppermute | solution.py:329
  20.2 0.0 collective-permute-done.7.far_ref
  20.2 2.3 %chain.1 = f32[4,16,512]{2,1,0:T(8,128)} custom-call(s32[8]{0:T(128)S(4)} %get-tuple-element.22.dir_ref, f32[8]{0:T(128)S(4)} %get-tuple-element.23.ext_ref, f32[8]{0:T(128)S(4)} %get-tuple-element.24.albedo_ref, f32[8,16,512]{2,1,0:T(8,128)S(1)} %get-tuple-element.25.lamp_ref, f32[20,16,512]{2,1,0:T(8,128)S(1)} %collective-permute-done.cells_ref.theirs_ref, ...), custom_call_target="tpu_custom_call" | custom-call | tf_op jit(solution)/shard_map/chain/pallas_call | solution.py:465
  (2 shorter events, 0.0 us)
Async XLA Ops:
  2.5 16.5 %collective-permute-start = (f32[20,16,512]{2,1,0:T(8,128)S(1)}, f32[20,16,512]{2,1,0:T(8,128)S(1)}, u32[]{:S(2)}, u32[]{:S(2)}) collective-permute-start(f32[20,16,512]{2,1,0:T(8,128)S(1)} %get-tuple-element.28), channel_id=1, source_target_pairs={{0,4},{4,0},{1,5},{5,1},{2,6},{6,2},{3,7},{7,3},{8,12},{12,8},{9,1... | collective-permute-start | bytes 1966088 | tf_op jit(solution)/shard_map/ppermute | solution.py:270
  3.0 4.2 %collective-permute-start.1 = (f32[16,128]{1,0:T(8,128)S(1)}, f32[16,128]{1,0:T(8,128)S(1)}, u32[]{:S(2)}, u32[]{:S(2)}) collective-permute-start(f32[16,128]{1,0:T(8,128)S(1)} %get-tuple-element.30), channel_id=1, source_target_pairs={{0,1},{1,2},{2,3},{3,11},{11,10},{10,9},{9,8},{8,0},{16,17},{17,18... | collective-permute-start | bytes 24584 | tf_op jit(solution)/shard_map/ppermute | solution.py:181
  5.7 3.7 %collective-permute-start.2 = (f32[16,128]{1,0:T(8,128)S(1)}, f32[16,128]{1,0:T(8,128)S(1)}, u32[]{:S(2)}, u32[]{:S(2)}) collective-permute-start(f32[16,128]{1,0:T(8,128)S(1)} %get-tuple-element.31), channel_id=1, source_target_pairs={{1,0},{2,1},{3,2},{11,3},{10,11},{9,10},{8,9},{0,8},{17,16},{18,17... | collective-permute-start | bytes 24584 | tf_op jit(solution)/shard_map/ppermute | solution.py:182
  9.3 5.0 %collective-permute-start.6 = (f32[16,640]{1,0:T(8,128)S(1)}, f32[16,640]{1,0:T(8,128)S(1)}, u32[]{:S(2)}, u32[]{:S(2)}) collective-permute-start(f32[16,640]{1,0:T(8,128)S(1)} %get-tuple-element.32), channel_id=1, source_target_pairs={{24,0},{16,8},{8,16},{0,24},{25,1},{17,9},{9,17},{1,25},{26,2},{18... | collective-permute-start | bytes 122888 | tf_op jit(solution)/shard_map/ppermute | solution.py:299
  10.8 4.0 %collective-permute-start.5 = (f32[16,640]{1,0:T(8,128)S(1)}, f32[16,640]{1,0:T(8,128)S(1)}, u32[]{:S(2)}, u32[]{:S(2)}) collective-permute-start(f32[16,640]{1,0:T(8,128)S(1)} %get-tuple-element.32), channel_id=1, source_target_pairs={{16,0},{24,8},{0,16},{8,24},{17,1},{25,9},{1,17},{9,25},{18,2},{26... | collective-permute-start | bytes 122888 | tf_op jit(solution)/shard_map/ppermute | solution.py:299
  14.8 5.4 %collective-permute-start.7 = (f32[48,640]{1,0:T(8,128)S(1)}, f32[48,640]{1,0:T(8,128)S(1)}, u32[]{:S(2)}, u32[]{:S(2)}) collective-permute-start(f32[48,640]{1,0:T(8,128)S(1)} %join.1.near_ref), channel_id=1, source_target_pairs={{0,4},{4,0},{1,5},{5,1},{2,6},{6,2},{3,7},{7,3},{8,12},{12,8},{9,1... | collective-permute-start | bytes 368648 | tf_op jit(solution)/shard_map/ppermute | solution.py:328
  14.9 4.1 %collective-permute-start.3 = (f32[16,640]{1,0:T(8,128)S(1)}, f32[16,640]{1,0:T(8,128)S(1)}, u32[]{:S(2)}, u32[]{:S(2)}) collective-permute-start(f32[16,640]{1,0:T(8,128)S(1)} %get-tuple-element.32), channel_id=1, source_target_pairs={{8,0},{0,8},{24,16},{16,24},{9,1},{1,9},{25,17},{17,25},{10,2},{2,... | collective-permute-start | bytes 122888 | tf_op jit(solution)/shard_map/ppermute | solution.py:299
  18.9 1.2 %collective-permute-start.4 = (f32[16,640]{1,0:T(8,128)S(1)}, f32[16,640]{1,0:T(8,128)S(1)}, u32[]{:S(2)}, u32[]{:S(2)}) collective-permute-start(f32[16,640]{1,0:T(8,128)S(1)} %collective-permute-done.3.near_last_ref), channel_id=1, source_target_pairs={{0,4},{4,0},{1,5},{5,1},{2,6},{6,2},{3,7},{7,3},{8,12},{12,8},{9,1... | collective-permute-start | bytes 122888 | tf_op jit(solution)/shard_map/ppermute | solution.py:329

commit v3 on v2

--- a/solution.py
+++ b/solution.py
@@ -23,14 +23,12 @@
     return steps
 
 
-def peer(position, k, count):
-    if count & (count - 1) == 0:
-        return position ^ k
-    return (position - k) % count
+def peer(position, k):
+    return position ^ k
 
 
 def light_pairs(k, count):
-    return [(peer(i, k, count), i) for i in range(count)]
+    return [(peer(i, k), i) for i in range(count)]
 
 
 def lane_iota(shape):
@@ -176,7 +174,7 @@
     )(*in_hbm(density, active_list, lamp_plane, light_dir, extinction, blur_weights, albedo))
 
     swap = [(0, 1), (1, 0)]
-    assert chain % 2 == 0
+    assert chain & (chain - 1) == 0 and chain > 2
     along = loops(chain, columns)
     got_along = lax.ppermute(edge_along, ("light", "height"), along)
     got_against = lax.ppermute(
@@ -307,16 +305,16 @@
         scratch_shapes=gains_scratch,
     )(*in_smem(dirs, exts), *in_vmem(theirs))
 
-    joined = (chain - 2) * depth_len
+    joined = (chain - 3) * depth_len
 
     def join_kernel(*refs):
         out_ref = refs[-1]
-        for k, ref in enumerate(refs[: chain - 2]):
+        for k, ref in enumerate(refs[: chain - 3]):
             out_ref[pl.ds(k * depth_len, depth_len), :] = ref[...]
         for t in range(2 * tiles):
             row, lane = divmod(t * LANES, wide)
             out_ref[pl.ds(joined + row * depth_len, depth_len), pl.ds(lane, LANES)] = refs[
-                chain - 2
+                chain - 3
             ][:, pl.ds(t * LANES, LANES)]
 
     parcel = pl.pallas_call(
@@ -324,37 +322,12 @@
         name="join",
         compiler_params=GRANT,
         out_shape=pltpu.VMEM((joined + halo_rows, wide), jnp.float32),
-    )(*in_vmem(*near[1:], halos))
+    )(*in_vmem(*near[2:], halos))
     far_parcel = lax.ppermute(parcel, "depth", swap)
+    far_side = lax.ppermute(near[1], "depth", swap)
     far_last = lax.ppermute(near[0], "depth", swap)
 
-    def chain_kernel(
-        dir_ref, ext_ref, albedo_ref, lamp_ref, theirs_ref, near_last_ref, far_last_ref,
-        near_ref, far_ref, taps_ref,
-        gain_near_ref, through_near_ref, gain_far_ref, through_far_ref, out_ref, walls, plane, lit,
-    ):
-        light = lax.axis_index("light")
-        depth = lax.axis_index("depth")
-        height = lax.axis_index("height")
-        own_row = pl.multiple_of(depth * depth_len, BZ)
-        other_row = pl.multiple_of((1 - depth) * depth_len, BZ)
-        for k in range(1, chain):
-            source = peer(light, k, chain)
-            for row, last, others in (
-                (own_row, near_last_ref, near_ref),
-                (other_row, far_last_ref, far_ref),
-            ):
-                if k > 1:
-                    column = others[pl.ds((k - 2) * depth_len, depth_len), :]
-                else:
-                    column = last[...]
-                walls[source, pl.ds(row, depth_len), :] = column
-        lane = lane_iota((depth_len, LANES))
-
-        def halo_tile(ref, t):
-            row, first = divmod(t * LANES, wide)
-            return ref[pl.ds(joined + row * depth_len, depth_len), pl.ds(first, LANES)]
-
+    def sorted_colours(dir_ref, depth):
         down = [dir_ref[depth * mine + i] for i in range(mine)]
         ups = mine - sum(down[1:], down[0])
         rank, ups_seen, downs_seen = [], 0, 0
@@ -366,6 +339,61 @@
             sum((jnp.where(rank[i] == r, i, 0) for i in range(1, mine)), jnp.int32(0))
             for r in range(mine)
         ]
+
+        def colour(at):
+            if isinstance(at, int):
+                return order[at]
+            c = order[0]
+            for i in range(1, mine):
+                c = jnp.where(at == i, order[i], c)
+            return c
+
+        return ups, rank, colour
+
+    def inside_lanes():
+        height = lax.axis_index("height")
+        wide_lane = lane_iota((1, wide))
+        inside = (
+            (wide_lane < height_len)
+            | ((wide_lane < height_len + LANES // 2) & (height < columns - 1))
+            | ((wide_lane >= height_len + LANES // 2) & (height > 0))
+        )
+        return jnp.where(inside, 1.0, 0.0)
+
+    def blurred(before, wall, rate, inside, taps):
+        high, low = split(before * (jnp.exp(-rate * wall) * inside))
+        bands = jnp.dot(
+            taps, jnp.concatenate([high, low, high], axis=0), preferred_element_type=jnp.float32
+        )
+        after = None
+        for b in range(TAPS):
+            part = bands[b * full : (b + 1) * full]
+            if b != TAPS // 2:
+                part = pltpu.roll(part, (TAPS // 2 - b) % wide, 1)
+            after = part if after is None else after + part
+        return after
+
+    def before_sides(length):
+        return length - length % 4 + jnp.where(length % 4 == 3, 1, 0)
+
+    def early_kernel(
+        dir_ref, ext_ref, lamp_ref, theirs_ref, near_ref, far_ref, taps_ref, plane, walls,
+    ):
+        light = lax.axis_index("light")
+        depth = lax.axis_index("depth")
+        own_row = pl.multiple_of(depth * depth_len, BZ)
+        other_row = pl.multiple_of((1 - depth) * depth_len, BZ)
+        for k in range(3, chain):
+            for row, ref in ((own_row, near_ref), (other_row, far_ref)):
+                column = ref[pl.ds((k - 3) * depth_len, depth_len), :]
+                walls[peer(light, k), pl.ds(row, depth_len), :] = column
+        lane = lane_iota((depth_len, LANES))
+
+        def halo_tile(ref, t):
+            row, first = divmod(t * LANES, wide)
+            return ref[pl.ds(joined + row * depth_len, depth_len), pl.ds(first, LANES)]
+
+        ups, rank, colour = sorted_colours(dir_ref, depth)
         for i in range(mine):
             for row, group, edges, body in (
                 (own_row, 1 + i, near_ref, lamp_ref[depth * mine + i]),
@@ -382,14 +410,9 @@
                 )
                 plane[rank[i], pl.ds(row, depth_len), pl.ds(0, height_len)] = body
                 plane[rank[i], pl.ds(row, depth_len), pl.ds(height_len, LANES)] = edge
-        wide_lane = lane_iota((1, wide))
-        inside = (
-            (wide_lane < height_len)
-            | ((wide_lane < height_len + LANES // 2) & (height < columns - 1))
-            | ((wide_lane >= height_len + LANES // 2) & (height > 0))
-        )
-        inside = jnp.where(inside, 1.0, 0.0)
-        ups_steps, down_steps = light, chain - 1 - light
+        inside = inside_lanes()
+        ups_steps = before_sides(light)
+        down_steps = before_sides(chain - 1 - light)
         shared = jnp.minimum(ups_steps, down_steps)
         longest = jnp.maximum(ups_steps, down_steps)
         ups_longer = ups_steps > down_steps
@@ -399,35 +422,16 @@
 
         def advance(places, s):
             results = []
-            for place_in in places:
-                c = depth * mine + order[place_in] if isinstance(place_in, int) else None
-                if c is None:
-                    c = depth * mine + chosen(place_in)
-                goes_down = place_in >= ups
+            for at in places:
+                c = colour(at)
+                goes_down = at >= ups
                 wall = walls[jnp.where(goes_down, chain - 1 - s, s)]
-                before = plane[place_in]
-                high, low = split(before * (jnp.exp(-ext_ref[c] * wall) * inside))
-                bands = jnp.dot(
-                    taps_ref[c - depth * mine],
-                    jnp.concatenate([high, low, high], axis=0),
-                    preferred_element_type=jnp.float32,
-                )
-                after = None
-                for b in range(TAPS):
-                    part = bands[b * full : (b + 1) * full]
-                    if b != TAPS // 2:
-                        part = pltpu.roll(part, (TAPS // 2 - b) % wide, 1)
-                    after = part if after is None else after + part
+                before = plane[at]
+                after = blurred(before, wall, ext_ref[depth * mine + c], inside, taps_ref[c])
                 active = s < jnp.where(goes_down, down_steps, ups_steps)
                 results.append(jnp.where(active, after, before))
-            for place_in, after in zip(places, results):
-                plane[place_in] = after
-
-        def chosen(place_in):
-            c = order[0]
-            for i in range(1, mine):
-                c = jnp.where(place_in == i, order[i], c)
-            return c
+            for at, after in zip(places, results):
+                plane[at] = after
 
         def all_step(s, carry):
             advance(range(mine), s)
@@ -438,9 +442,110 @@
             return carry
 
         lax.fori_loop(0, jnp.where(as_pair, shared, longest), all_step, 0)
-        lax.fori_loop(
-            shared, jnp.where(as_pair & (alone > 0), longest, shared), pair_step, 0
-        )
+        lax.fori_loop(shared, jnp.where(as_pair & (alone > 0), longest, shared), pair_step, 0)
+
+    planes = pl.pallas_call(
+        early_kernel,
+        name="early",
+        compiler_params=GRANT,
+        in_specs=[SMEM] * 2 + [VMEM] * 5,
+        out_shape=pltpu.VMEM((mine, full, wide), jnp.float32),
+        scratch_shapes=[pltpu.VMEM((chain, full, wide), jnp.float32)],
+    )(*in_smem(dirs, exts), *in_vmem(lamps, theirs, parcel, far_parcel, taps))
+
+    def middle_kernel(
+        dir_ref, ext_ref, planes_ref, near_ref, far_ref, side_ref, far_side_ref, taps_ref, plane, walls,
+    ):
+        light = lax.axis_index("light")
+        depth = lax.axis_index("depth")
+        own_row = pl.multiple_of(depth * depth_len, BZ)
+        other_row = pl.multiple_of((1 - depth) * depth_len, BZ)
+        walls[0, pl.ds(own_row, depth_len), :] = side_ref[...]
+        walls[0, pl.ds(other_row, depth_len), :] = far_side_ref[...]
+        walls[1, pl.ds(own_row, depth_len), :] = near_ref[pl.ds(0, depth_len), :]
+        walls[1, pl.ds(other_row, depth_len), :] = far_ref[pl.ds(0, depth_len), :]
+        ups, _, colour = sorted_colours(dir_ref, depth)
+        inside = inside_lanes()
+        ups_move = light % 4 >= 2
+        length = jnp.where(ups_move, light, chain - 1 - light)
+        start = before_sides(length)
+        end = length - length % 2
+        moving = jnp.where(ups_move, ups, mine - ups)
+        first = jnp.where(ups_move, 0, ups)
+        for i in range(mine):
+            plane[i] = planes_ref[i]
+
+        def advance(places, s):
+            source = jnp.where(ups_move, s, chain - 1 - s)
+            wall = walls[peer(light, source) - 2]
+            results = []
+            for at in places:
+                c = colour(at)
+                before = plane[at]
+                after = blurred(before, wall, ext_ref[depth * mine + c], inside, taps_ref[c])
+                moves = (at >= first) & (at < first + moving)
+                results.append(jnp.where(moves, after, before))
+            for at, after in zip(places, results):
+                plane[at] = after
+
+        def all_step(s, carry):
+            advance(range(mine), s)
+            return carry
+
+        def pair_step(s, carry):
+            advance((first, first + jnp.maximum(moving - 1, 0)), s)
+            return carry
+
+        few = moving <= 2
+        lax.fori_loop(start, jnp.where(few & (moving > 0), end, start), pair_step, 0)
+        lax.fori_loop(start, jnp.where(few, start, end), all_step, 0)
+
+    planes = pl.pallas_call(
+        middle_kernel,
+        name="middle",
+        compiler_params=GRANT,
+        in_specs=[SMEM] * 2 + [VMEM] * 6,
+        out_shape=pltpu.VMEM((mine, full, wide), jnp.float32),
+        scratch_shapes=[pltpu.VMEM((2, full, wide), jnp.float32)],
+    )(*in_smem(dirs, exts), *in_vmem(planes, parcel, far_parcel, near[1], far_side, taps))
+
+    def late_kernel(
+        dir_ref, ext_ref, albedo_ref, planes_ref, last_ref, far_last_ref, taps_ref,
+        gain_near_ref, through_near_ref, gain_far_ref, through_far_ref, out_ref, plane, wall, lit,
+    ):
+        light = lax.axis_index("light")
+        depth = lax.axis_index("depth")
+        own_row = pl.multiple_of(depth * depth_len, BZ)
+        other_row = pl.multiple_of((1 - depth) * depth_len, BZ)
+        wall[pl.ds(own_row, depth_len), :] = last_ref[...]
+        wall[pl.ds(other_row, depth_len), :] = far_last_ref[...]
+        ups, rank, colour = sorted_colours(dir_ref, depth)
+        inside = inside_lanes()
+        ups_move = light % 2 == 1
+        moving = jnp.where(ups_move, ups, mine - ups)
+        first = jnp.where(ups_move, 0, ups)
+        for i in range(mine):
+            plane[i] = planes_ref[i]
+
+        def advance(places):
+            results = []
+            for at in places:
+                c = colour(at)
+                before = planes_ref[at]
+                after = blurred(before, wall[...], ext_ref[depth * mine + c], inside, taps_ref[c])
+                moves = (at >= first) & (at < first + moving)
+                results.append(jnp.where(moves, after, before))
+            for at, after in zip(places, results):
+                plane[at] = after
+
+        @pl.when((moving > 0) & (moving <= 2))
+        def _():
+            advance((first, first + moving - 1))
+
+        @pl.when(moving > 2)
+        def _():
+            advance(range(mine))
+
         in_front = depth == 0
         for i in range(mine):
             for half, row in enumerate((own_row, other_row)):
@@ -463,20 +568,20 @@
                 out_ref[i, :, span] = shade * (front + through * back)
 
     return pl.pallas_call(
-        chain_kernel,
-        name="chain",
-        compiler_params=GRANT,
-        in_specs=[SMEM] * 3 + [VMEM] * 11,
+        late_kernel,
+        name="late",
+        compiler_params=GRANT,
+        in_specs=[SMEM] * 3 + [VMEM] * 8,
         out_specs=VMEM,
         out_shape=jax.ShapeDtypeStruct((mine, slices, height_len), jnp.float32),
         scratch_shapes=[
-            pltpu.VMEM((chain, full, wide), jnp.float32),
             pltpu.VMEM((mine, full, wide), jnp.float32),
+            pltpu.VMEM((full, wide), jnp.float32),
             pltpu.VMEM((groups, mine, depth_len, height_len), jnp.float32),
         ],
     )(
         *in_smem(dirs, exts, albedos),
-        *in_vmem(lamps, theirs, near[0], far_last, parcel, far_parcel, taps),
+        *in_vmem(planes, near[0], far_last, taps),
         *in_vmem(gain_near, through_near, gain_far, through_far),
     )
 

time: 22.6 us -> 23.4 us (1.035)
  waiting for transfers between devices: 10.2 us -> 10.7 us
    ppermute x3, waiting for transfers between devices: 6.23 us -> 7.04 us  [local(): near.append(lax.ppermute(wide_column, 'light', light_pairs(k, chain)))]
    ppermute x1, waiting for transfers between devices: 0.27 us -> 0.01 us  [local(): far_last = lax.ppermute(near[0], 'depth', swap)]
    pallas_call x1 -> x3, Pallas kernels: 2.3 us -> 2.4 us  [the longest x1 1.43 us: local(): pl.pallas_call(late_kernel, name='late', compiler_params=GRANT, in_specs=...]
  transfers between devices with their start and end apart: 8 -> 9, of which waited for: 6 -> 5; matrix products, arithmetic and copies ran while one was open for 0% -> 0% of each run, Pallas kernels for 4% -> 8%
where the time goes in v3:
time: 23.4 us; the launch traced here: 23.3 us
  waiting for transfers between devices  10.7 us (46%)
  starting transfers between devices  6.7 us (29%)
  Pallas kernels  5.81 us (25%)
    ppermute x3, waiting for transfers between devices, local(): near.append(lax.ppermute(wide_column, 'light', light_pairs(k, chain)))  7.04 us
    ppermute x3, starting transfers between devices, local(): near.append(lax.ppermute(wide_column, 'light', light_pairs(k, chain)))  3.5 us
    ppermute x1, starting transfers between devices, local(): got_along = lax.ppermute(edge_along, ('light', 'height'), along)  2.62 us
    ppermute x1, waiting for transfers between devices, local(): lax.ppermute(edge_against, ('light', 'height'), [(target, source) for sou...  2.11 us
    ppermute x1, waiting for transfers between devices, local(): got_along = lax.ppermute(edge_along, ('light', 'height'), along)  1.54 us
    pallas_call x1, Pallas kernels, local(): pl.pallas_call(late_kernel, name='late', compiler_params=GRANT, in_specs=...  1.43 us
    pallas_call x1, Pallas kernels, local(): pl.pallas_call(sums_kernel, name='sums', compiler_params=GRANT, in_specs=...  1.32 us
    pallas_call x1, Pallas kernels, local(): pl.pallas_call(near_kernel, name='near_gains', compiler_params=GRANT, in_...  1.13 us
  transfers between devices with their start and end apart: 9, of which 5 were waited for; matrix products, arithmetic and copies ran while one was open for 0% of the time, Pallas kernels for 8%

profile of v3, /device:TPU:0, one launch (start us, length us, event | category | flops | bytes accessed | tf_op | source)
XLA Modules:
  0.0 23.3 jit_solution(13295240468661260232)
XLA Ops:
  0.0 1.3 %sums.1 = (f32[16,16,512]{2,1,0:T(8,128)S(1)}, f32[16,512]{1,0:T(8,128)S(1)}, f32[16,128]{1,0:T(8,128)S(1)}, f32[16,128]{1,0:T(8,128)S(1)}, f32[8,16,512]{2,1,0:...) custom-call(f32[16,16,512]{2,1,0:T(8,128)} %density_hbm.1, ...), custom_call_target="tpu_custom_call" | custom-call | tf_op jit(solution)/shard_map/sums/pallas_call | solution.py:152
  1.3 1.1 %near_gains.1 = (f32[4,16,16,512]{3,2,1,0:T(8,128)S(1)}, f32[16,512]{1,0:T(8,128)S(1)}, bf16[4,160,96]{2,1,0:T(8,128)(2,1)S(1)}, f32[20,16,512]{2,1,0:T(8,128)S(1)}) custom-call(s32[8]{0:T(128)S(4)} %get-tuple-element.22.dir_ref, f32[8]{0:T(128)S(4)} %get-tuple-element.23.ext_ref, f32[8,25]{1,0:T(8,128)S(4)} %get-tuple-element.26.blur_ref, ...), custom_call_target="tpu_custom_call" | custom-call | tf_op jit(solution)/shard_map/near_gains/pallas_call | solution.py:255
  2.5 0.6 %collective-permute-start = (f32[20,16,512]{2,1,0:T(8,128)S(1)}, f32[20,16,512]{2,1,0:T(8,128)S(1)}, u32[]{:S(2)}, u32[]{:S(2)}) collective-permute-start(f32[20,16,512]{2,1,0:T(8,128)S(1)} %get-tuple-element.28), channel_id=1, source_target_pairs={{0,4},{4,0},{1,5},{5,1},{2,6},{6,2},{3,7},{7,3},{8,12},{12,8},{9,1... | collective-permute-start | bytes 1966088 | tf_op jit(solution)/shard_map/ppermute | solution.py:268
  3.0 2.6 %collective-permute-start.1 = (f32[16,128]{1,0:T(8,128)S(1)}, f32[16,128]{1,0:T(8,128)S(1)}, u32[]{:S(2)}, u32[]{:S(2)}) collective-permute-start(f32[16,128]{1,0:T(8,128)S(1)} %get-tuple-element.30), channel_id=1, source_target_pairs={{0,1},{1,2},{2,3},{3,11},{11,10},{10,9},{9,8},{8,0},{16,17},{17,18... | collective-permute-start | bytes 24584 | tf_op jit(solution)/shard_map/ppermute | solution.py:179
  5.7 0.0 collective-permute-start.2
  5.7 1.5 %collective-permute-done.1.along_ref = f32[16,128]{1,0:T(8,128)S(1)} collective-permute-done((f32[16,128]{1,0:T(8,128)S(1)}, f32[16,128]{1,0:T(8,128)S(1)}, u32[]{:S(2)}, u32[]{:S(2)}) %collective-permute-start.1) | collective-permute-done | bytes 8224 | tf_op jit(solution)/shard_map/ppermute | solution.py:179
  7.2 2.1 %collective-permute-done.2.against_ref = f32[16,128]{1,0:T(8,128)S(1)} collective-permute-done((f32[16,128]{1,0:T(8,128)S(1)}, f32[16,128]{1,0:T(8,128)S(1)}, u32[]{:S(2)}, u32[]{:S(2)}) %collective-permute-start.2) | collective-permute-done | bytes 8224 | tf_op jit(solution)/shard_map/ppermute | solution.py:180
  9.3 1.5 %collective-permute-start.3 = (f32[16,640]{1,0:T(8,128)S(1)}, f32[16,640]{1,0:T(8,128)S(1)}, u32[]{:S(2)}, u32[]{:S(2)}) collective-permute-start(f32[16,640]{1,0:T(8,128)S(1)} %get-tuple-element.32), channel_id=1, source_target_pairs={{24,0},{16,8},{8,16},{0,24},{25,1},{17,9},{9,17},{1,25},{26,2},{18... | collective-permute-start | bytes 122888 | tf_op jit(solution)/shard_map/ppermute | solution.py:297
  10.8 3.5 %collective-permute-done.3.refs_0_ = f32[16,640]{1,0:T(8,128)S(1)} collective-permute-done((f32[16,640]{1,0:T(8,128)S(1)}, f32[16,640]{1,0:T(8,128)S(1)}, u32[]{:S(2)}, u32[]{:S(2)}) %collective-permute-start.3) | collective-permute-done | bytes 40992 | tf_op jit(solution)/shard_map/ppermute | solution.py:297
  14.3 0.0 collective-permute-start.4
  14.3 1.6 %collective-permute-start.5 = (f32[16,640]{1,0:T(8,128)S(1)}, f32[16,640]{1,0:T(8,128)S(1)}, u32[]{:S(2)}, u32[]{:S(2)}) collective-permute-start(f32[16,640]{1,0:T(8,128)S(1)} %get-tuple-element.32), channel_id=1, source_target_pairs={{16,0},{24,8},{0,16},{8,24},{17,1},{25,9},{1,17},{9,25},{18,2},{26... | collective-permute-start | bytes 122888 | tf_op jit(solution)/shard_map/ppermute | solution.py:297
  15.9 0.4 %collective-permute-start.7 = (f32[16,640]{1,0:T(8,128)S(1)}, f32[16,640]{1,0:T(8,128)S(1)}, u32[]{:S(2)}, u32[]{:S(2)}) collective-permute-start(f32[16,640]{1,0:T(8,128)S(1)} %get-tuple-element.32), channel_id=1, source_target_pairs={{8,0},{0,8},{24,16},{16,24},{9,1},{1,9},{25,17},{17,25},{10,2},{2,... | collective-permute-start | bytes 122888 | tf_op jit(solution)/shard_map/ppermute | solution.py:297
  16.3 2.0 %collective-permute-done.5.side_ref = f32[16,640]{1,0:T(8,128)S(1)} collective-permute-done((f32[16,640]{1,0:T(8,128)S(1)}, f32[16,640]{1,0:T(8,128)S(1)}, u32[]{:S(2)}, u32[]{:S(2)}) %collective-permute-start.5) | collective-permute-done | bytes 40992 | tf_op jit(solution)/shard_map/ppermute | solution.py:297
  18.4 0.0 collective-permute-start.6
  18.4 1.5 %collective-permute-done.7.last_ref = f32[16,640]{1,0:T(8,128)S(1)} collective-permute-done((f32[16,640]{1,0:T(8,128)S(1)}, f32[16,640]{1,0:T(8,128)S(1)}, u32[]{:S(2)}, u32[]{:S(2)}) %collective-permute-start.7) | collective-permute-done | bytes 40992 | tf_op jit(solution)/shard_map/ppermute | solution.py:297
  19.9 0.0 collective-permute-start.8
  19.9 0.0 collective-permute-done.theirs_ref.cells_ref
  19.9 0.9 %far_gains.1 = (f32[4,16,16,512]{3,2,1,0:T(8,128)S(1)}, f32[16,512]{1,0:T(8,128)S(1)}) custom-call(s32[8]{0:T(128)S(4)} %get-tuple-element.22.dir_ref, f32[8]{0:T(128)S(4)} %get-tuple-element.23.ext_ref, f32[20,16,512]{2,1,0:T(8,128)S(1)} %collective-permute-done.theirs_ref.cells_ref), custom_call_target="tpu_custom_call" | custom-call | tf_op jit(solution)/shard_map/far_gains/pallas_call | solution.py:299
  20.8 0.0 collective-permute-done.4.far_ref
  20.8 0.5 %early.1.planes_ref = f32[4,32,640]{2,1,0:T(8,128)S(1)} custom-call(s32[8]{0:T(128)S(4)} %get-tuple-element.22.dir_ref, f32[8]{0:T(128)S(4)} %get-tuple-element.23.ext_ref, f32[8,16,512]{2,1,0:T(8,128)S(1)} %get-tuple-element.25.lamp_ref, f32[20,16,512]{2,1,0:T(8,128)S(1)} %collective-permute-done.theirs_ref.cells_ref, f32[32,640]{1,0:T(8,128)S(1)} %join.1.near_ref, ...), custom_call_target="tpu_custom_call" | custom-call | tf_op jit(solution)/shard_map/early/pallas_call | solution.py:447
  21.4 0.0 collective-permute-done.6.far_side_ref
  21.4 0.5 %middle.1.planes_ref = f32[4,32,640]{2,1,0:T(8,128)S(1)} custom-call(s32[8]{0:T(128)S(4)} %get-tuple-element.22.dir_ref, f32[8]{0:T(128)S(4)} %get-tuple-element.23.ext_ref, f32[4,32,640]{2,1,0:T(8,128)S(1)} %early.1.planes_ref, f32[32,640]{1,0:T(8,128)S(1)} %join.1.near_ref, f32[32,640]{1,0:T(8,128)S(1)} %collective-permute-done.4.far_ref, ...), custom_call_target="tpu_custom_call" | custom-call | tf_op jit(solution)/shard_map/middle/pallas_call | solution.py:503
  21.8 0.0 collective-permute-done.8.far_last_ref
  21.9 1.4 %late.1 = f32[4,16,512]{2,1,0:T(8,128)} custom-call(s32[8]{0:T(128)S(4)} %get-tuple-element.22.dir_ref, f32[8]{0:T(128)S(4)} %get-tuple-element.23.ext_ref, f32[8]{0:T(128)S(4)} %get-tuple-element.24.albedo_ref, f32[4,32,640]{2,1,0:T(8,128)S(1)} %middle.1.planes_ref, f32[16,640]{1,0:T(8,128)S(1)} %collective-permute-done.7.last_ref, ...), custom_call_target="tpu_custom_call" | custom-call | tf_op jit(solution)/shard_map/late/pallas_call | solution.py:570
  (2 shorter events, 0.0 us)
Async XLA Ops:
  2.5 17.4 %collective-permute-start = (f32[20,16,512]{2,1,0:T(8,128)S(1)}, f32[20,16,512]{2,1,0:T(8,128)S(1)}, u32[]{:S(2)}, u32[]{:S(2)}) collective-permute-start(f32[20,16,512]{2,1,0:T(8,128)S(1)} %get-tuple-element.28), channel_id=1, source_target_pairs={{0,4},{4,0},{1,5},{5,1},{2,6},{6,2},{3,7},{7,3},{8,12},{12,8},{9,1... | collective-permute-start | bytes 1966088 | tf_op jit(solution)/shard_map/ppermute | solution.py:268
  3.0 4.2 %collective-permute-start.1 = (f32[16,128]{1,0:T(8,128)S(1)}, f32[16,128]{1,0:T(8,128)S(1)}, u32[]{:S(2)}, u32[]{:S(2)}) collective-permute-start(f32[16,128]{1,0:T(8,128)S(1)} %get-tuple-element.30), channel_id=1, source_target_pairs={{0,1},{1,2},{2,3},{3,11},{11,10},{10,9},{9,8},{8,0},{16,17},{17,18... | collective-permute-start | bytes 24584 | tf_op jit(solution)/shard_map/ppermute | solution.py:179
  5.7 3.7 %collective-permute-start.2 = (f32[16,128]{1,0:T(8,128)S(1)}, f32[16,128]{1,0:T(8,128)S(1)}, u32[]{:S(2)}, u32[]{:S(2)}) collective-permute-start(f32[16,128]{1,0:T(8,128)S(1)} %get-tuple-element.31), channel_id=1, source_target_pairs={{1,0},{2,1},{3,2},{11,3},{10,11},{9,10},{8,9},{0,8},{17,16},{18,17... | collective-permute-start | bytes 24584 | tf_op jit(solution)/shard_map/ppermute | solution.py:180
  9.3 5.0 %collective-permute-start.3 = (f32[16,640]{1,0:T(8,128)S(1)}, f32[16,640]{1,0:T(8,128)S(1)}, u32[]{:S(2)}, u32[]{:S(2)}) collective-permute-start(f32[16,640]{1,0:T(8,128)S(1)} %get-tuple-element.32), channel_id=1, source_target_pairs={{24,0},{16,8},{8,16},{0,24},{25,1},{17,9},{9,17},{1,25},{26,2},{18... | collective-permute-start | bytes 122888 | tf_op jit(solution)/shard_map/ppermute | solution.py:297
  14.3 6.5 %collective-permute-start.4 = (f32[32,640]{1,0:T(8,128)S(1)}, f32[32,640]{1,0:T(8,128)S(1)}, u32[]{:S(2)}, u32[]{:S(2)}) collective-permute-start(f32[32,640]{1,0:T(8,128)S(1)} %join.1.near_ref), channel_id=1, source_target_pairs={{0,4},{4,0},{1,5},{5,1},{2,6},{6,2},{3,7},{7,3},{8,12},{12,8},{9,1... | collective-permute-start | bytes 245768 | tf_op jit(solution)/shard_map/ppermute | solution.py:326
  14.3 4.1 %collective-permute-start.5 = (f32[16,640]{1,0:T(8,128)S(1)}, f32[16,640]{1,0:T(8,128)S(1)}, u32[]{:S(2)}, u32[]{:S(2)}) collective-permute-start(f32[16,640]{1,0:T(8,128)S(1)} %get-tuple-element.32), channel_id=1, source_target_pairs={{16,0},{24,8},{0,16},{8,24},{17,1},{25,9},{1,17},{9,25},{18,2},{26... | collective-permute-start | bytes 122888 | tf_op jit(solution)/shard_map/ppermute | solution.py:297
  15.9 4.0 %collective-permute-start.7 = (f32[16,640]{1,0:T(8,128)S(1)}, f32[16,640]{1,0:T(8,128)S(1)}, u32[]{:S(2)}, u32[]{:S(2)}) collective-permute-start(f32[16,640]{1,0:T(8,128)S(1)} %get-tuple-element.32), channel_id=1, source_target_pairs={{8,0},{0,8},{24,16},{16,24},{9,1},{1,9},{25,17},{17,25},{10,2},{2,... | collective-permute-start | bytes 122888 | tf_op jit(solution)/shard_map/ppermute | solution.py:297
  18.4 3.0 %collective-permute-start.6 = (f32[16,640]{1,0:T(8,128)S(1)}, f32[16,640]{1,0:T(8,128)S(1)}, u32[]{:S(2)}, u32[]{:S(2)}) collective-permute-start(f32[16,640]{1,0:T(8,128)S(1)} %collective-permute-done.5.side_ref), channel_id=1, source_target_pairs={{0,4},{4,0},{1,5},{5,1},{2,6},{6,2},{3,7},{7,3},{8,12},{12,8},{9,1... | collective-permute-start | bytes 122888 | tf_op jit(solution)/shard_map/ppermute | solution.py:327
  19.9 2.0 %collective-permute-start.8 = (f32[16,640]{1,0:T(8,128)S(1)}, f32[16,640]{1,0:T(8,128)S(1)}, u32[]{:S(2)}, u32[]{:S(2)}) collective-permute-start(f32[16,640]{1,0:T(8,128)S(1)} %collective-permute-done.7.last_ref), channel_id=1, source_target_pairs={{0,4},{4,0},{1,5},{5,1},{2,6},{6,2},{3,7},{7,3},{8,12},{12,8},{9,1... | collective-permute-start | bytes 122888 | tf_op jit(solution)/shard_map/ppermute | solution.py:328
